TPU v7x, 32 devices: a whole 2x2x4 slice. The times are simulated.
32 devices in a mesh: wide: 16 (over z, y, x), narrow: 2 (over core).
Axes of the slice: x: 2, y: 2, z: 4, core: 2. Of those that a mesh axis runs over, the one named last changes fastest.
Arguments:
- pressure: float32 [128, 128, 512], P('wide', 'narrow'), may hold values from -6 to 6
Outputs:
- detail_one: float32 [7, 64, 64, 256], P(None, 'wide', 'narrow')
- detail_two: float32 [7, 32, 32, 128], P(None, 'wide', 'narrow')
- detail_three: float32 [7, 16, 16, 64], P(None, 'wide', 'narrow')
- bands_four: float32 [8, 8, 8, 32], P(None, None, 'narrow')
All inputs are finite; a program needn't handle non-finite values.
Results may differ from a plain program's by a relative error of at most 0.00016.
Values sent between devices are 32-bit elements; how exact they have to be, the bound alone decides.
No kernel may reach another device: no remote copies, remote signals or barrier semaphores. Data moves between devices by JAX's collectives and lax.ppermute only.
A program may use at most 64 MiB of HBM per device.

v0:
```python
import numpy as np

import jax
import jax.numpy as jnp
from jax import lax
from jax.experimental import pallas as pl
from jax.experimental.pallas import tpu as pltpu
from jax.sharding import PartitionSpec as P


ALPHA = -1.586134342
BETA = -0.05298011854
GAMMA = 0.8829110762
DELTA = 0.4435068522
ZETA = 1.149604398

LANES = 128
SUB = 8
HALO = 16
PARTS = 2
EDGE = 4
BASE = 24
F32 = jnp.float32
VMEM_LIMIT = 16 * 1024 * 1024
VMEM = pl.BlockSpec(memory_space=pltpu.VMEM)


def lift_table(size):
    cells = np.eye(size)
    even, odd = cells[:, 0::2].copy(), cells[:, 1::2].copy()

    def ahead(v):
        return np.concatenate([v[:, 1:], v[:, -1:]], 1)

    def behind(v):
        return np.concatenate([v[:, :1], v[:, :-1]], 1)

    odd += ALPHA * (even + ahead(even))
    even += BETA * (behind(odd) + odd)
    odd += GAMMA * (even + ahead(even))
    even += DELTA * (behind(odd) + odd)
    return np.concatenate([even * ZETA, odd / ZETA], 1)


def lift_taps():
    table = lift_table(32)
    low, high = table[:, 8], table[:, 16 + 8]
    return [float(low[16 + t]) for t in range(5)], [float(high[17 + t]) for t in range(4)]


LOW, HIGH = lift_taps()


def np_split(table):
    import ml_dtypes

    whole = np.asarray(table, np.float32)
    top = whole.astype(ml_dtypes.bfloat16)
    rest = (whole - top.astype(np.float32)).astype(ml_dtypes.bfloat16)
    return jnp.asarray(top), jnp.asarray(rest)


def halves(v):
    top = v.astype(jnp.bfloat16)
    return top, (v - top.astype(F32)).astype(jnp.bfloat16)


def dot3(v, th, tl):
    top, rest = v
    return (
        jnp.dot(top, th, preferred_element_type=F32)
        + jnp.dot(top, tl, preferred_element_type=F32)
        + jnp.dot(rest, th, preferred_element_type=F32)
    )


def taps_low(at):
    return LOW[0] * at(0) + (
        (LOW[1] * (at(-1) + at(1)) + LOW[2] * (at(-2) + at(2)))
        + (LOW[3] * (at(-3) + at(3)) + LOW[4] * (at(-4) + at(4)))
    )


def taps_high(at):
    return (HIGH[0] * at(1) + HIGH[1] * (at(0) + at(2))) + (
        HIGH[2] * (at(-1) + at(3)) + HIGH[3] * (at(-2) + at(4))
    )


def z_right(s, d):
    return d[-1] + ALPHA * s[-1], s[-1] + BETA * (d[-2] + ALPHA * (s[-2] + s[-1]))


def z_left(s, d):
    return s[0], d[0] + ALPHA * (s[0] + s[1])


def z_lift(s, d, left, right, first, last):
    m = len(s)
    s0p = jnp.where(last, s[-1], right[0])
    d1 = [d[i] + ALPHA * (s[i] + (s[i + 1] if i + 1 < m else s0p)) for i in range(m)]
    d1m = jnp.where(first, d1[0], left[0] + ALPHA * s[0])
    s1 = [s[i] + BETA * ((d1[i - 1] if i else d1m) + d1[i]) for i in range(m)]
    s1p = jnp.where(last, s1[-1], s0p + BETA * (d1[-1] + right[1]))
    d2 = [d1[i] + GAMMA * (s1[i] + (s1[i + 1] if i + 1 < m else s1p)) for i in range(m)]
    s1m = left[1] + BETA * d1m
    d2m = jnp.where(first, d2[0], d1m + GAMMA * (s1m + s1[0]))
    s2 = [s1[i] + DELTA * ((d2[i - 1] if i else d2m) + d2[i]) for i in range(m)]
    return [v * ZETA for v in s2], [v * (1.0 / ZETA) for v in d2]


def place(axis):
    me, count = lax.axis_index(axis), lax.axis_size(axis)
    return me, me == 0, me == count - 1


def spread(value, th_ref, tl_ref, store):
    nz, rows, nx = value.shape
    parts = halves(value.reshape(nz * rows, nx))
    step = 2 * LANES
    for n in range(0, nx, step):
        got = dot3(parts, th_ref[:, n : n + step], tl_ref[:, n : n + step]).reshape(nz, rows, step)
        for k in range(step // LANES):
            store(n // LANES + k, got[:, :, k * LANES : (k + 1) * LANES])


def x_one(x_hbm, th_hbm, tl_hbm, xs, th_ref, tl_ref, xv, sems):
    nz, ny, _ = xv.shape
    part = nz // PARTS
    tables = [
        pltpu.make_async_copy(th_hbm, th_ref, sems.at[PARTS]),
        pltpu.make_async_copy(tl_hbm, tl_ref, sems.at[PARTS + 1]),
    ]
    pieces = [
        pltpu.make_async_copy(x_hbm.at[pl.ds(k * part, part)], xv.at[pl.ds(k * part, part)], sems.at[k])
        for k in range(PARTS)
    ]
    for copy in [pieces[0]] + tables + pieces[1:]:
        copy.start()
    for copy in tables:
        copy.wait()
    for k in range(PARTS):
        pieces[k].wait()
        planes = slice(k * part, (k + 1) * part)

        def store(chunk, block):
            xs[planes, chunk, BASE : BASE + ny, :] = block

        spread(xv[planes], th_ref, tl_ref, store)


def xy_one(*refs, one_halo):
    n_halo = 1 if one_halo else 2
    x_ref, halo_refs = refs[0], refs[1 : 1 + n_halo]
    th_ref, tl_ref, xs, ll_ref, d_ref, le_ref, lo_ref, de_ref, do_ref = refs[1 + n_halo :]
    nz, chunks, tall, _ = x_ref.shape
    ny = tall - 2 * BASE
    cl = chunks // 2
    own = ny // 2
    _, first, last = place("narrow")
    even = lax.rem(lax.axis_index("wide"), 2) == 0

    top, bottom = BASE - HALO, BASE + ny

    def store_at(starts):
        def store(chunk, block):
            for start in starts:
                xs[:, chunk, start : start + HALO, :] = block

        return store

    if one_halo:
        begin = pl.multiple_of(jnp.where(first, 0, ny - HALO), HALO)
        spread(halo_refs[0][:, pl.ds(begin, HALO), :], th_ref, tl_ref, store_at((top, bottom)))
    else:
        spread(halo_refs[0][...], th_ref, tl_ref, store_at((top,)))
        spread(halo_refs[1][...], th_ref, tl_ref, store_at((bottom,)))

    @pl.when(first)
    def _():
        for t in range(1, 13):
            upto = cl if t > EDGE else 2 * cl
            xs[:, :upto, BASE - t : BASE - t + 1, :] = xs[:, :upto, BASE + t : BASE + t + 1, :]

    end = BASE + ny - 1

    @pl.when(last)
    def _():
        for t in range(1, EDGE + 1):
            xs[:, :, end + t : end + t + 1, :] = xs[:, :, end - t : end - t + 1, :]

    upper = lax.broadcasted_iota(jnp.int32, (SUB, LANES), 0) < EDGE

    @pl.loop(0, nz)
    def _(p):
        for c in range(cl):

            def rows(chunk, start, n):
                return lambda t: xs[p, chunk, pl.ds(start + t, n, stride=2), :]

            ll_ref[p, c, :own, :] = taps_low(rows(c, BASE, own))
            below = taps_low(rows(c, BASE + ny, SUB))
            above = taps_low(rows(c, BASE - 2 * SUB, SUB))
            ll_ref[p, c, own : own + SUB, :] = jnp.where(upper, below, above)
            d_ref[0, p, c] = taps_low(rows(cl + c, BASE, own))
            d_ref[1, p, c] = taps_high(rows(c, BASE, own))
            d_ref[2, p, c] = taps_high(rows(cl + c, BASE, own))

    @pl.when(last)
    def _():
        for t in range(1, EDGE + 1):
            at = own - 1
            ll_ref[:, :, at + t : at + t + 1, :] = ll_ref[:, :, at - t : at - t + 1, :]

    def edges(plane):
        s = [plane(0), plane(2), plane(nz - 4), plane(nz - 2)]
        d = [plane(1), None, plane(nz - 3), plane(nz - 1)]
        return z_right(s, d), z_left(s, d)

    for c in range(cl):
        right, left = edges(lambda k: ll_ref[k, c])
        for j in range(2):
            le_ref[j, c] = jnp.where(even, right[j], left[j])
            lo_ref[j, c] = jnp.where(even, left[j], right[j])
        for b in range(3):
            right, left = edges(lambda k: d_ref[b, k, c])
            for j in range(2):
                de_ref[b, j, c] = jnp.where(even, right[j], left[j])
                do_ref[b, j, c] = jnp.where(even, left[j], right[j])


def xy_two(ll_ref, re_ref, ro_ref, th_ref, tl_ref, g_ref, d2_ref, h_ref, pe_ref, po_ref, lw, ys):
    nz, cl, tall, _ = ll_ref.shape
    own = tall - SUB
    m = nz // 2
    half = own // 2
    me, first, last = place("wide")
    even = lax.rem(me, 2) == 0
    for c in range(cl):
        s = [ll_ref[2 * i, c] for i in range(m)]
        d = [ll_ref[2 * i + 1, c] for i in range(m)]
        left = [jnp.where(even, ro_ref[j, c], re_ref[j, c]) for j in range(2)]
        right = [jnp.where(even, re_ref[j, c], ro_ref[j, c]) for j in range(2)]
        low, high = z_lift(s, d, left, right, first, last)
        for i in range(m):
            lw[i, :, c * LANES : (c + 1) * LANES] = low[i]
            h_ref[i, c] = high[i][:own]
    got = dot3(halves(lw[...].reshape(m * tall, cl * LANES)), th_ref[...], tl_ref[...])
    got = got.reshape(m, tall, 2 * LANES)
    for xb in range(2):
        part = got[:, :, xb * LANES : (xb + 1) * LANES]
        ys[:, xb, SUB : SUB + own, :] = part[:, :own]
        ys[:, xb, :SUB, :] = part[:, own:]
        ys[:, xb, SUB + own : 2 * SUB + own, :] = part[:, own:]
    for i in range(m):

        def rows(xb):
            return lambda t: ys[i, xb, pl.ds(SUB + t, half, stride=2), :]

        g_ref[i] = taps_low(rows(0))
        d2_ref[0, i] = taps_low(rows(1))
        d2_ref[1, i] = taps_high(rows(0))
        d2_ref[2, i] = taps_high(rows(1))
    for b in range(3):
        s = [d2_ref[b, 2 * i] for i in range(m // 2)]
        d = [d2_ref[b, 2 * i + 1] for i in range(m // 2)]
        right, left = z_right(s, d), z_left(s, d)
        for j in range(2):
            pe_ref[b, j] = jnp.where(even, right[j], left[j])
            po_ref[b, j] = jnp.where(even, left[j], right[j])


def halo_lift(plane, count, got_e, got_o):
    me, first, last = place("wide")
    even = lax.rem(me, 2) == 0
    s = [plane(2 * i) for i in range(count)]
    d = [plane(2 * i + 1) for i in range(count)]
    left = [jnp.where(even, got_o(j), got_e(j)) for j in range(2)]
    right = [jnp.where(even, got_e(j), got_o(j)) for j in range(2)]
    return z_lift(s, d, left, right, first, last)


def z_one(d_ref, re_ref, ro_ref, h_ref, one_ref):
    _, nz, cl, _, _ = d_ref.shape
    m = nz // 2
    for c in range(cl):
        lanes = slice(c * LANES, (c + 1) * LANES)
        for i in range(m):
            one_ref[3, i, :, lanes] = h_ref[i, c]
        for b in range(3):
            low, high = halo_lift(
                lambda k: d_ref[b, k, c], m, lambda j: re_ref[b, j, c], lambda j: ro_ref[b, j, c]
            )
            for i in range(m):
                one_ref[b, i, :, lanes] = low[i]
                one_ref[4 + b, i, :, lanes] = high[i]


def z_two(d_ref, re_ref, ro_ref, h_ref, two_ref):
    m = d_ref.shape[1] // 2
    for i in range(m):
        two_ref[3, i] = h_ref[i]
    for b in range(3):
        low, high = halo_lift(lambda k: d_ref[b, k], m, lambda j: re_ref[b, j], lambda j: ro_ref[b, j])
        for i in range(m):
            two_ref[b, i] = low[i]
            two_ref[4 + b, i] = high[i]


def mirrored(j, size):
    if isinstance(j, int):
        return -j if j < 0 else (2 * (size - 1) - j if j >= size else j)
    return jnp.where(j < 0, -j, jnp.where(j >= size, 2 * (size - 1) - j, j))


def z_deep(*refs, slots):
    got_refs = refs[: len(slots)]
    h2_ref, zz_ref, seq, low2, low3 = refs[len(slots) :]
    m = got_refs[0].shape[-3]
    me = lax.axis_index("wide")
    for ref, offsets in zip(got_refs, slots):
        for k, offset in enumerate(offsets):
            chip = lax.bitwise_xor(me, offset)
            piece = ref[k] if len(ref.shape) == 4 else ref[...]
            seq[pl.ds(chip * m, m)] = piece
    size = seq.shape[0]

    def at_of(ref, size, i):
        return lambda t: ref[mirrored(2 * i + t, size)]

    for i in range(size // 2):
        low2[i] = taps_low(at_of(seq, size, i))
    for i in range(m // 2):
        h2_ref[i] = taps_high(at_of(seq, size, me * (m // 2) + i))
    size2 = size // 2
    for i in range(size2 // 2):
        low3[i] = taps_low(at_of(low2, size2, i))
    own3 = m // 4
    size3 = size2 // 2
    for i in range(own3):
        zz_ref[i] = low3[me * own3 + i]
        zz_ref[own3 + i] = taps_high(at_of(low2, size2, me * own3 + i))
    for i in range(size3 // 2):
        zz_ref[2 * own3 + i] = taps_low(at_of(low3, size3, i))
        zz_ref[2 * own3 + size3 // 2 + i] = taps_high(at_of(low3, size3, i))


def pick(me, value, count):
    rows = value.shape[0] // count
    out = value[:rows]
    for k in range(1, count):
        out = jnp.where(me == k, value[k * rows : (k + 1) * rows], out)
    return out


def xy_deep(*refs, pair, own3):
    if pair:
        zz_ref, other_ref = refs[:2]
    else:
        zz_ref = refs[0]
    th3, tl3, th4, tl4, three_ref, four_ref, xs, ys = refs[2 if pair else 1 :]
    me = lax.axis_index("narrow")
    count = lax.axis_size("narrow")
    planes, rows = zz_ref.shape[-3], zz_ref.shape[-2]
    full = rows * count

    def put(value, start):
        a = 2 * own3
        got = dot3(halves(value[:a].reshape(a * rows, LANES)), th3[...], tl3[...])
        xs[:a, pl.ds(start, rows), :] = got.reshape(a, rows, LANES)
        b = planes - a
        got = dot3(halves(value[a:].reshape(b * rows, LANES)), th4[...], tl4[...])
        xs[a:, pl.ds(start, rows), :] = got.reshape(b, rows, LANES)

    if pair:
        put(zz_ref[...], pl.multiple_of(SUB + rows * me, SUB))
        put(other_ref[...], pl.multiple_of(SUB + rows * (1 - me), SUB))
    else:
        for k in range(count):
            put(zz_ref[k], SUB + rows * k)

    def fold(ref, size):
        end = SUB + size - 1
        for t in range(1, EDGE + 1):
            ref[:, SUB - t : SUB - t + 1, :] = ref[:, SUB + t : SUB + t + 1, :]
            ref[:, end + t : end + t + 1, :] = ref[:, end - t : end - t + 1, :]

    fold(xs, full)
    n3 = full // 2
    wide3 = three_ref.shape[-1]
    for k in range(2 * own3):
        bz, i = k // own3, k % own3
        at = lambda t: xs[k, pl.ds(SUB + t, n3, stride=2), :]
        for by, taps in enumerate((taps_low, taps_high)):
            mine = pick(me, taps(at), count)
            for bx in range(2):
                band = 4 * bz + 2 * by + bx
                if band:
                    three_ref[band - 1, i] = mine[:, bx * wide3 : (bx + 1) * wide3]
    for k in range(2 * own3, planes):
        at = lambda t: xs[k, pl.ds(SUB + t, n3, stride=2), :]
        ys[k - 2 * own3, SUB : SUB + n3, :] = taps_low(at)
    fold(ys, n3)
    n4 = n3 // 2
    wide4 = four_ref.shape[-1]
    deep = (planes - 2 * own3) // 2
    for k in range(2 * deep):
        bz, i = k // deep, k % deep
        at = lambda t: ys[k, pl.ds(SUB + t, n4, stride=2), :]
        for by, taps in enumerate((taps_low, taps_high)):
            mine = pick(me, taps(at), count)
            for bx in range(2):
                four_ref[4 * bz + 2 * by + bx, i] = mine[:, bx * wide4 : (bx + 1) * wide4]


def call(kernel, outs, scratch, cost=2_000_000, aliases=None):
    return pl.pallas_call(
        kernel,
        out_shape=tuple(jax.ShapeDtypeStruct(shape, F32) for shape in outs),
        out_specs=tuple(VMEM for _ in outs),
        scratch_shapes=[pltpu.VMEM(shape, F32) for shape in scratch],
        cost_estimate=pl.CostEstimate(flops=cost, bytes_accessed=cost, transcendentals=0),
        compiler_params=pltpu.CompilerParams(vmem_limit_bytes=VMEM_LIMIT),
        input_output_aliases=aliases or {},
    )


def wide_swap(value, partner):
    count = lax.axis_size("wide")
    return lax.ppermute(value, "wide", [(i, partner(i)) for i in range(count) if 0 <= partner(i) < count])


def even_pair(i):
    return i ^ 1


def odd_pair(i):
    return ((i + 1) ^ 1) - 1


def xor_pair(mask):
    return lambda i: i ^ mask


def gather_stages(count):
    bits = count.bit_length() - 1
    stages = []
    while bits > 0:
        take = 2 if bits >= 2 else 1
        bits -= take
        stages.append([k << bits for k in range(1, 1 << take)])
    return stages


def per_device(pressure):
    nz, ny, nx = pressure.shape
    count_y = lax.axis_size("narrow")
    count_z = lax.axis_size("wide")
    cl = nx // 2 // LANES
    own = ny // 2
    if count_y == 2:
        halos = (lax.ppermute(pressure, "narrow", [(0, 1), (1, 0)]),)
    else:
        head, tail = pressure[:, :HALO], pressure[:, ny - HALO :]
        halos = (
            lax.ppermute(tail, "narrow", [(i, i + 1) for i in range(count_y - 1)]),
            lax.ppermute(head, "narrow", [(i + 1, i) for i in range(count_y - 1)]),
        )
    table = np_split(lift_table(nx))
    padded = (nz, 2 * cl, ny + 2 * BASE, LANES)
    hbm = pl.BlockSpec(memory_space=pltpu.HBM)
    x_own, *table = pl.pallas_call(
        x_one,
        out_shape=(jax.ShapeDtypeStruct(padded, F32),)
        + tuple(jax.ShapeDtypeStruct(part.shape, part.dtype) for part in table),
        in_specs=(hbm, hbm, hbm),
        out_specs=(VMEM, VMEM, VMEM),
        scratch_shapes=[pltpu.VMEM((nz, ny, nx), F32), pltpu.SemaphoreType.DMA((PARTS + 2,))],
        cost_estimate=pl.CostEstimate(flops=2_000_000, bytes_accessed=2_000_000, transcendentals=0),
        compiler_params=pltpu.CompilerParams(vmem_limit_bytes=VMEM_LIMIT),
        name="x_one",
    )(*[pltpu.with_memory_space_constraint(v, pltpu.HBM) for v in (pressure, *table)])
    _, ll, d, le, lo, de, do = call(
        lambda *refs: xy_one(*refs, one_halo=count_y == 2),
        [
            padded,
            (nz, cl, own + SUB, LANES),
            (3, nz, cl, own, LANES),
            (2, cl, own + SUB, LANES),
            (2, cl, own + SUB, LANES),
            (3, 2, cl, own, LANES),
            (3, 2, cl, own, LANES),
        ],
        [],
        aliases={0: 0},
    )(x_own, *halos, *table)
    re = wide_swap(le, even_pair)
    ro = wide_swap(lo, odd_pair)
    rde = wide_swap(de, even_pair)
    rdo = wide_swap(do, odd_pair)
    m, half = nz // 2, own // 2
    g, d2, h, pe, po = call(
        xy_two,
        [
            (m, half, LANES),
            (3, m, half, LANES),
            (m, cl, own, LANES),
            (3, 2, half, LANES),
            (3, 2, half, LANES),
        ],
        [(m, own + SUB, cl * LANES), (m, 2, own + 2 * SUB, LANES)],
    )(ll, re, ro, *np_split(lift_table(nx // 2)))
    pieces, slots = [g], [[0]]
    stages = gather_stages(count_z)
    for n, masks in enumerate(stages):
        if n:
            whole = jnp.concatenate([p.reshape((-1, m, half, LANES)) for p in pieces], 0)
            flat = [o for part in slots for o in part]
        else:
            whole, flat = g, [0]
        pieces = [whole]
        for mask in masks:
            pieces.append(wide_swap(whole, xor_pair(mask)))
        slots = [flat] + [[o ^ mask for o in flat] for mask in masks]
    re2 = wide_swap(pe, even_pair)
    ro2 = wide_swap(po, odd_pair)
    size = m * count_z
    own3 = m // 4
    planes = 2 * own3 + size // 4
    h2, zz = call(
        lambda *refs: z_deep(*refs, slots=slots),
        [(m // 2, half, LANES), (planes, half, LANES)],
        [(size, half, LANES), (size // 2, half, LANES), (size // 4, half, LANES)],
    )(*pieces)
    (detail_one,) = call(z_one, [(7, m, own, cl * LANES)], [])(d, rde, rdo, h)
    (detail_two,) = call(z_two, [(7, m // 2, half, LANES)], [])(d2, re2, ro2, h2)
    table3 = lift_table(nx // 4)
    table4 = table3[:, : nx // 8] @ lift_table(nx // 8)
    table4 = np.concatenate([table4, np.zeros((nx // 4, LANES - nx // 8))], 1)
    if count_y == 2:
        rest = (zz, lax.ppermute(zz, "narrow", [(0, 1), (1, 0)]))
    else:
        rest = (lax.all_gather(zz, "narrow"),)
    full = half * count_y
    detail_three, bands_four = call(
        lambda *refs: xy_deep(*refs, pair=count_y == 2, own3=own3),
        [(7, own3, half // 2, nx // 8), (8, size // 8, half // 4, nx // 16)],
        [(planes, full + 2 * SUB, LANES), (planes - 2 * own3, full // 2 + 2 * SUB, LANES)],
    )(*rest, *np_split(table3), *np_split(table4))
    return detail_one, detail_two, detail_three, bands_four


def solution(mesh):
    in_specs = (P("wide", "narrow", None),)
    out_specs = (
        P(None, "wide", "narrow", None),
        P(None, "wide", "narrow", None),
        P(None, "wide", "narrow", None),
        P(None, None, "narrow", None),
    )

    return jax.shard_map(per_device, mesh=mesh, in_specs=in_specs, out_specs=out_specs, check_vma=False)
```

profile of v0, /device:TPU:14, one launch (start us, length us, event | category | flops | bytes accessed | tf_op | source)
XLA Modules:
  0.0 44.7 jit_solution(8247214534042662117)
XLA Ops:
  0.6 0.1 collective-permute-start
  0.7 2.5 %x_one.1 = (f32[8,4,112,128]{3,2,1,0:T(8,128)S(1)}, bf16[512,512]{1,0:T(8,128)(2,1)S(1)}, bf16[512,512]{1,0:T(8,128)(2,1)S(1)}) custom-call(f32[8,64,512]{2,1,0:T(8,128)} %x_hbm.1, bf16[512,512]{1,0:T(8,128)(2,1)} %constant.16.clone.th_hbm, bf16[512,512]{1,0:T(8,128)(2,1)} %constant.17.clone.tl_hbm), custom_call_target="tpu_custom_call" | custom-call | flops 2000000 | bytes 2000000 | tf_op jit(solution)/shard_map/x_one/pallas_call | solution.py:472
  3.3 0.3 collective-permute-done.refs_1_
  3.6 0.0 copy-start
  3.6 0.0 copy-start.1
  3.6 1.1 %shard_map.120 = (f32[8,4,112,128]{3,2,1,0:T(8,128)S(1)}, f32[8,2,40,128]{3,2,1,0:T(8,128)S(1)}, f32[3,8,2,32,128]{4,3,2,1,0:T(8,128)S(1)}, f32[2,2,40,128]{3,2,...) custom-call(f32[8,4,112,128]{3,2,1,0:T(8,128)S(1)} %get-tuple-elemen, ...), custom_call_target="tpu_custom_call", output_to_operand_aliasing={{0}: (0, {})} | custom-call | flops 2000000 | bytes 2000000 | tf_op jit(solution)/shard_map/pallas_call | solution.py:483
  4.7 0.6 %collective-permute-start.3 = (f32[2,2,40,128]{3,2,1,0:T(8,128)S(1)}, f32[2,2,40,128]{3,2,1,0:T(8,128)S(1)}, u32[]{:S(2)}, u32[]{:S(2)}) collective-permute-start(f32[2,2,40,128]{3,2,1,0:T(8,128)S(1)} %get-tuple-element.29), channel_id=1, source_target_pairs={{0,2},{2,0},{4,6},{6,4},{8,10},{10,8},{12,14},{14,12},{16,18},{18,... | collective-permute-start | bytes 245768 | tf_op jit(solution)/shard_map/ppermute | solution.py:430
  5.3 4.3 %collective-permute-start.4 = (f32[2,2,40,128]{3,2,1,0:T(8,128)S(1)}, f32[2,2,40,128]{3,2,1,0:T(8,128)S(1)}, u32[]{:S(2)}, u32[]{:S(2)}) collective-permute-start(f32[2,2,40,128]{3,2,1,0:T(8,128)S(1)} %get-tuple-element.30), channel_id=1, source_target_pairs={{2,4},{4,2},{6,8},{8,6},{10,12},{12,10},{14,16},{16,14},{18,20},{2... | collective-permute-start | bytes 245768 | tf_op jit(solution)/shard_map/ppermute | solution.py:430
  9.6 0.0 collective-permute-done.3.re_ref
  9.7 3.8 %collective-permute-done.4.ro_ref = f32[2,2,40,128]{3,2,1,0:T(8,128)S(1)} collective-permute-done((f32[2,2,40,128]{3,2,1,0:T(8,128)S(1)}, f32[2,2,40,128]{3,2,1,0:T(8,128)S(1)}, u32[]{:S(2)}, u32[]{:S(2)}) %collective-permute-start.4) | collective-permute-done | bytes 81952 | tf_op jit(solution)/shard_map/ppermute | solution.py:430
  13.4 0.0 copy-done
  13.4 0.0 copy-done.1
  13.4 0.4 shard_map.121
  13.8 0.0 copy-start.2
  13.8 0.0 copy-start.3
  13.8 0.0 copy-start.4
  13.8 0.0 copy-start.5
  13.8 1.6 %collective-permute-start.9 = (f32[4,16,128]{2,1,0:T(8,128)S(1)}, f32[4,16,128]{2,1,0:T(8,128)S(1)}, u32[]{:S(2)}, u32[]{:S(2)}) collective-permute-start(f32[4,16,128]{2,1,0:T(8,128)S(1)} %get-tuple-element.35), channel_id=1, source_target_pairs={{0,24},{2,26},{4,28},{6,30},{8,16},{10,18},{12,20},{14,22},{16,8},... | collective-permute-start | bytes 98312 | tf_op jit(solution)/shard_map/ppermute | solution.py:430
  15.5 1.2 %collective-permute-start.8 = (f32[4,16,128]{2,1,0:T(8,128)S(1)}, f32[4,16,128]{2,1,0:T(8,128)S(1)}, u32[]{:S(2)}, u32[]{:S(2)}) collective-permute-start(f32[4,16,128]{2,1,0:T(8,128)S(1)} %get-tuple-element.35), channel_id=1, source_target_pairs={{0,16},{2,18},{4,20},{6,22},{8,24},{10,26},{12,28},{14,30},{16,0},... | collective-permute-start | bytes 98312 | tf_op jit(solution)/shard_map/ppermute | solution.py:430
  16.7 0.7 %collective-permute-start.7 = (f32[4,16,128]{2,1,0:T(8,128)S(1)}, f32[4,16,128]{2,1,0:T(8,128)S(1)}, u32[]{:S(2)}, u32[]{:S(2)}) collective-permute-start(f32[4,16,128]{2,1,0:T(8,128)S(1)} %get-tuple-element.35), channel_id=1, source_target_pairs={{0,8},{2,10},{4,12},{6,14},{8,0},{10,2},{12,4},{14,6},{16,24},{18,... | collective-permute-start | bytes 98312 | tf_op jit(solution)/shard_map/ppermute | solution.py:430
  17.4 0.8 %collective-permute-done.9 = f32[4,16,128]{2,1,0:T(8,128)S(1)} collective-permute-done((f32[4,16,128]{2,1,0:T(8,128)S(1)}, f32[4,16,128]{2,1,0:T(8,128)S(1)}, u32[]{:S(2)}, u32[]{:S(2)}) %collective-permute-start.9) | collective-permute-done | bytes 32800 | tf_op jit(solution)/shard_map/ppermute | solution.py:430
  18.2 2.1 %collective-permute-done.8 = f32[4,16,128]{2,1,0:T(8,128)S(1)} collective-permute-done((f32[4,16,128]{2,1,0:T(8,128)S(1)}, f32[4,16,128]{2,1,0:T(8,128)S(1)}, u32[]{:S(2)}, u32[]{:S(2)}) %collective-permute-start.8) | collective-permute-done | bytes 32800 | tf_op jit(solution)/shard_map/ppermute | solution.py:430
  20.3 0.3 collective-permute-done.7
  20.6 1.4 %collective-permute-start.12 = (f32[4,4,16,128]{3,2,1,0:T(8,128)S(1)}, f32[4,4,16,128]{3,2,1,0:T(8,128)S(1)}, u32[]{:S(2)}, u32[]{:S(2)}) collective-permute-start(f32[4,4,16,128]{3,2,1,0:T(8,128)S(1)} %pad_maximum_fusion.refs_0_), channel_id=1, source_target_pairs={{0,6},{2,4},{4,2},{6,0},{8,14},{10,12},{12,10},{14,8},{16,22},{18,... | collective-permute-start | bytes 393224 | tf_op jit(solution)/shard_map/ppermute | solution.py:430
  22.0 0.7 %collective-permute-start.11 = (f32[4,4,16,128]{3,2,1,0:T(8,128)S(1)}, f32[4,4,16,128]{3,2,1,0:T(8,128)S(1)}, u32[]{:S(2)}, u32[]{:S(2)}) collective-permute-start(f32[4,4,16,128]{3,2,1,0:T(8,128)S(1)} %pad_maximum_fusion.refs_0_), channel_id=1, source_target_pairs={{0,4},{2,6},{4,0},{6,2},{8,12},{10,14},{12,8},{14,10},{16,20},{18,... | collective-permute-start | bytes 393224 | tf_op jit(solution)/shard_map/ppermute | solution.py:430
  22.8 1.4 %collective-permute-start.10 = (f32[4,4,16,128]{3,2,1,0:T(8,128)S(1)}, f32[4,4,16,128]{3,2,1,0:T(8,128)S(1)}, u32[]{:S(2)}, u32[]{:S(2)}) collective-permute-start(f32[4,4,16,128]{3,2,1,0:T(8,128)S(1)} %pad_maximum_fusion.refs_0_), channel_id=1, source_target_pairs={{0,2},{2,0},{4,6},{6,4},{8,10},{10,8},{12,14},{14,12},{16,18},{18,... | collective-permute-start | bytes 393224 | tf_op jit(solution)/shard_map/ppermute | solution.py:430
  24.2 0.6 %collective-permute-start.1 = (f32[3,2,2,32,128]{4,3,2,1,0:T(8,128)S(1)}, f32[3,2,2,32,128]{4,3,2,1,0:T(8,128)S(1)}, u32[]{:S(2)}, u32[]{:S(2)}) collective-permute-start(f32[3,2,2,32,128]{4,3,2,1,0:T(8,128)S(1)} %get-tuple-element.26), channel_id=1, source_target_pairs={{0,2},{2,0},{4,6},{6,4},{8,10},{10,8},{12,14},{14,12},{16,18},{18,... | collective-permute-start | bytes 589832 | tf_op jit(solution)/shard_map/ppermute | solution.py:430
  24.8 4.9 %collective-permute-start.2 = (f32[3,2,2,32,128]{4,3,2,1,0:T(8,128)S(1)}, f32[3,2,2,32,128]{4,3,2,1,0:T(8,128)S(1)}, u32[]{:S(2)}, u32[]{:S(2)}) collective-permute-start(f32[3,2,2,32,128]{4,3,2,1,0:T(8,128)S(1)} %get-tuple-element.27), channel_id=1, source_target_pairs={{2,4},{4,2},{6,8},{8,6},{10,12},{12,10},{14,16},{16,14},{18,20},{2... | collective-permute-start | bytes 589832 | tf_op jit(solution)/shard_map/ppermute | solution.py:430
  29.7 0.4 collective-permute-done.12.refs_3_
  30.1 0.2 collective-permute-done.11.refs_2_
  30.3 1.8 %collective-permute-done.10.refs_1_ = f32[4,4,16,128]{3,2,1,0:T(8,128)S(1)} collective-permute-done((f32[4,4,16,128]{3,2,1,0:T(8,128)S(1)}, f32[4,4,16,128]{3,2,1,0:T(8,128)S(1)}, u32[]{:S(2)}, u32[]{:S(2)}) %collective-permute-start.10) | collective-permute-done | bytes 131104 | tf_op jit(solution)/shard_map/ppermute | solution.py:430
  32.1 0.3 shard_map.123
  32.4 0.1 collective-permute-start.13
  32.4 2.5 %collective-permute-start.5 = (f32[3,2,16,128]{3,2,1,0:T(8,128)S(1)}, f32[3,2,16,128]{3,2,1,0:T(8,128)S(1)}, u32[]{:S(2)}, u32[]{:S(2)}) collective-permute-start(f32[3,2,16,128]{3,2,1,0:T(8,128)S(1)} %get-tuple-element.33), channel_id=1, source_target_pairs={{0,2},{2,0},{4,6},{6,4},{8,10},{10,8},{12,14},{14,12},{16,18},{18,... | collective-permute-start | bytes 147464 | tf_op jit(solution)/shard_map/ppermute | solution.py:430
  35.0 2.7 %collective-permute-start.6 = (f32[3,2,16,128]{3,2,1,0:T(8,128)S(1)}, f32[3,2,16,128]{3,2,1,0:T(8,128)S(1)}, u32[]{:S(2)}, u32[]{:S(2)}) collective-permute-start(f32[3,2,16,128]{3,2,1,0:T(8,128)S(1)} %get-tuple-element.34), channel_id=1, source_target_pairs={{2,4},{4,2},{6,8},{8,6},{10,12},{12,10},{14,16},{16,14},{18,20},{2... | collective-permute-start | bytes 147464 | tf_op jit(solution)/shard_map/ppermute | solution.py:430
  37.7 0.0 collective-permute-done.1.re_ref
  37.7 0.0 collective-permute-done.2.ro_ref
  37.7 1.2 %shard_map.122 = f32[7,4,32,256]{3,2,1,0:T(8,128)} custom-call(f32[3,8,2,32,128]{4,3,2,1,0:T(8,128)S(1)} %get-tuple-element.25.d_ref, f32[3,2,2,32,128]{4,3,2,1,0:T(8,128)S(1)} %collective-permute-done.1.re_ref, f32[3,2,2,32,128]{4,3,2,1,0:T(8,128)S(1)} %collective-permute-done.2.ro_ref, f32[4,2,32,128]{3,2,1,0:T(8,128)S(1)} %get-tuple-element.31.h_ref), custom_call_target="tpu_custom_call" | custom-call | flops 2000000 | bytes 2000000 | tf_op jit(solution)/shard_map/pallas_call | solution.py:535
  38.9 0.0 collective-permute-done.5.re_ref
  38.9 3.9 %collective-permute-done.6.ro_ref = f32[3,2,16,128]{3,2,1,0:T(8,128)S(1)} collective-permute-done((f32[3,2,16,128]{3,2,1,0:T(8,128)S(1)}, f32[3,2,16,128]{3,2,1,0:T(8,128)S(1)}, u32[]{:S(2)}, u32[]{:S(2)}) %collective-permute-start.6) | collective-permute-done | bytes 49184 | tf_op jit(solution)/shard_map/ppermute | solution.py:430
  42.7 0.7 %shard_map.124 = f32[7,2,16,128]{3,2,1,0:T(8,128)} custom-call(f32[3,4,16,128]{3,2,1,0:T(8,128)S(1)} %get-tuple-element.32.d_ref, f32[3,2,16,128]{3,2,1,0:T(8,128)S(1)} %collective-permute-done.5.re_ref, f32[3,2,16,128]{3,2,1,0:T(8,128)S(1)} %collective-permute-done.6.ro_ref, f32[2,16,128]{2,1,0:T(8,128)S(1)} %get-tuple-element.36.h_ref), custom_call_target="tpu_custom_call" | custom-call | flops 2000000 | bytes 2000000 | tf_op jit(solution)/shard_map/pallas_call | solution.py:536
  43.4 0.0 collective-permute-done.13.refs_1_
  43.4 0.0 copy-done.2
  43.4 0.0 copy-done.3
  43.4 0.0 copy-done.4
  43.4 0.0 copy-done.5
  43.5 1.3 %shard_map.125 = (f32[7,1,8,64]{3,2,1,0:T(8,128)}, f32[8,8,4,32]{3,2,1,0:T(4,128)}) custom-call(f32[18,16,128]{2,1,0:T(8,128)S(1)} %get-tuple-element.37.refs_0_, f32[18,16,128]{2,1,0:T(8,128)S(1)} %collective-permute-done.13.refs_1_, bf16[128,128]{1,0:T(8,128)(2,1)S(1)} %copy-done.5, bf16[128,128]{1,0:T(8,128)(2,1)S(1)} %copy-done.4, ...), custom_call_target="tpu_custom_call" | custom-call | flops 2000000 | bytes 2000000 | tf_op jit(solution)/shard_map/pallas_call | solution.py:545
  (1 shorter events, 0.0 us)
Async XLA Ops:
  0.6 2.9 %collective-permute-start = (f32[8,64,512]{2,1,0:T(8,128)}, f32[8,64,512]{2,1,0:T(8,128)S(1)}, u32[]{:S(2)}, u32[]{:S(2)}) collective-permute-start(f32[8,64,512]{2,1,0:T(8,128)} %x_hbm.1), channel_id=1, source_target_pairs={{0,1},{1,0},{2,3},{3,2},{4,5},{5,4},{6,7},{7,6},{8,9},{9,8},{10,11... | collective-permute-start | bytes 3145736 | tf_op jit(solution)/shard_map/ppermute | solution.py:462
  3.6 9.8 %copy-start = (bf16[256,256]{1,0:T(8,128)(2,1)S(1)}, bf16[256,256]{1,0:T(8,128)(2,1)}, u32[]{:S(2)}) copy-start(bf16[256,256]{1,0:T(8,128)(2,1)} %constant.19.clone.tl_ref) | copy-start | bytes 393220
  3.6 9.8 %copy-start.1 = (bf16[256,256]{1,0:T(8,128)(2,1)S(1)}, bf16[256,256]{1,0:T(8,128)(2,1)}, u32[]{:S(2)}) copy-start(bf16[256,256]{1,0:T(8,128)(2,1)} %constant.18.clone.th_ref) | copy-start | bytes 393220
  4.7 5.0 %collective-permute-start.3 = (f32[2,2,40,128]{3,2,1,0:T(8,128)S(1)}, f32[2,2,40,128]{3,2,1,0:T(8,128)S(1)}, u32[]{:S(2)}, u32[]{:S(2)}) collective-permute-start(f32[2,2,40,128]{3,2,1,0:T(8,128)S(1)} %get-tuple-element.29), channel_id=1, source_target_pairs={{0,2},{2,0},{4,6},{6,4},{8,10},{10,8},{12,14},{14,12},{16,18},{18,... | collective-permute-start | bytes 245768 | tf_op jit(solution)/shard_map/ppermute | solution.py:430
  5.3 8.1 %collective-permute-start.4 = (f32[2,2,40,128]{3,2,1,0:T(8,128)S(1)}, f32[2,2,40,128]{3,2,1,0:T(8,128)S(1)}, u32[]{:S(2)}, u32[]{:S(2)}) collective-permute-start(f32[2,2,40,128]{3,2,1,0:T(8,128)S(1)} %get-tuple-element.30), channel_id=1, source_target_pairs={{2,4},{4,2},{6,8},{8,6},{10,12},{12,10},{14,16},{16,14},{18,20},{2... | collective-permute-start | bytes 245768 | tf_op jit(solution)/shard_map/ppermute | solution.py:430
  13.8 29.7 %copy-start.2 = (bf16[128,128]{1,0:T(8,128)(2,1)S(1)}, bf16[128,128]{1,0:T(8,128)(2,1)}, u32[]{:S(2)}) copy-start(bf16[128,128]{1,0:T(8,128)(2,1)} %constant.23.clone.refs_5_) | copy-start | bytes 98308
  13.8 29.6 %copy-start.3 = (bf16[128,128]{1,0:T(8,128)(2,1)S(1)}, bf16[128,128]{1,0:T(8,128)(2,1)}, u32[]{:S(2)}) copy-start(bf16[128,128]{1,0:T(8,128)(2,1)} %constant.22.clone.refs_4_) | copy-start | bytes 98308
  13.8 29.6 %copy-start.4 = (bf16[128,128]{1,0:T(8,128)(2,1)S(1)}, bf16[128,128]{1,0:T(8,128)(2,1)}, u32[]{:S(2)}) copy-start(bf16[128,128]{1,0:T(8,128)(2,1)} %constant.21.clone.refs_3_) | copy-start | bytes 98308
  13.8 29.6 %copy-start.5 = (bf16[128,128]{1,0:T(8,128)(2,1)S(1)}, bf16[128,128]{1,0:T(8,128)(2,1)}, u32[]{:S(2)}) copy-start(bf16[128,128]{1,0:T(8,128)(2,1)} %constant.20.clone.refs_2_) | copy-start | bytes 98308
  13.8 4.3 %collective-permute-start.9 = (f32[4,16,128]{2,1,0:T(8,128)S(1)}, f32[4,16,128]{2,1,0:T(8,128)S(1)}, u32[]{:S(2)}, u32[]{:S(2)}) collective-permute-start(f32[4,16,128]{2,1,0:T(8,128)S(1)} %get-tuple-element.35), channel_id=1, source_target_pairs={{0,24},{2,26},{4,28},{6,30},{8,16},{10,18},{12,20},{14,22},{16,8},... | collective-permute-start | bytes 98312 | tf_op jit(solution)/shard_map/ppermute | solution.py:430
  15.5 4.8 %collective-permute-start.8 = (f32[4,16,128]{2,1,0:T(8,128)S(1)}, f32[4,16,128]{2,1,0:T(8,128)S(1)}, u32[]{:S(2)}, u32[]{:S(2)}) collective-permute-start(f32[4,16,128]{2,1,0:T(8,128)S(1)} %get-tuple-element.35), channel_id=1, source_target_pairs={{0,16},{2,18},{4,20},{6,22},{8,24},{10,26},{12,28},{14,30},{16,0},... | collective-permute-start | bytes 98312 | tf_op jit(solution)/shard_map/ppermute | solution.py:430
  16.7 3.9 %collective-permute-start.7 = (f32[4,16,128]{2,1,0:T(8,128)S(1)}, f32[4,16,128]{2,1,0:T(8,128)S(1)}, u32[]{:S(2)}, u32[]{:S(2)}) collective-permute-start(f32[4,16,128]{2,1,0:T(8,128)S(1)} %get-tuple-element.35), channel_id=1, source_target_pairs={{0,8},{2,10},{4,12},{6,14},{8,0},{10,2},{12,4},{14,6},{16,24},{18,... | collective-permute-start | bytes 98312 | tf_op jit(solution)/shard_map/ppermute | solution.py:430
  20.6 9.4 %collective-permute-start.12 = (f32[4,4,16,128]{3,2,1,0:T(8,128)S(1)}, f32[4,4,16,128]{3,2,1,0:T(8,128)S(1)}, u32[]{:S(2)}, u32[]{:S(2)}) collective-permute-start(f32[4,4,16,128]{3,2,1,0:T(8,128)S(1)} %pad_maximum_fusion.refs_0_), channel_id=1, source_target_pairs={{0,6},{2,4},{4,2},{6,0},{8,14},{10,12},{12,10},{14,8},{16,22},{18,... | collective-permute-start | bytes 393224 | tf_op jit(solution)/shard_map/ppermute | solution.py:430
  22.0 8.3 %collective-permute-start.11 = (f32[4,4,16,128]{3,2,1,0:T(8,128)S(1)}, f32[4,4,16,128]{3,2,1,0:T(8,128)S(1)}, u32[]{:S(2)}, u32[]{:S(2)}) collective-permute-start(f32[4,4,16,128]{3,2,1,0:T(8,128)S(1)} %pad_maximum_fusion.refs_0_), channel_id=1, source_target_pairs={{0,4},{2,6},{4,0},{6,2},{8,12},{10,14},{12,8},{14,10},{16,20},{18,... | collective-permute-start | bytes 393224 | tf_op jit(solution)/shard_map/ppermute | solution.py:430
  22.8 9.3 %collective-permute-start.10 = (f32[4,4,16,128]{3,2,1,0:T(8,128)S(1)}, f32[4,4,16,128]{3,2,1,0:T(8,128)S(1)}, u32[]{:S(2)}, u32[]{:S(2)}) collective-permute-start(f32[4,4,16,128]{3,2,1,0:T(8,128)S(1)} %pad_maximum_fusion.refs_0_), channel_id=1, source_target_pairs={{0,2},{2,0},{4,6},{6,4},{8,10},{10,8},{12,14},{14,12},{16,18},{18,... | collective-permute-start | bytes 393224 | tf_op jit(solution)/shard_map/ppermute | solution.py:430
  24.2 13.5 %collective-permute-start.1 = (f32[3,2,2,32,128]{4,3,2,1,0:T(8,128)S(1)}, f32[3,2,2,32,128]{4,3,2,1,0:T(8,128)S(1)}, u32[]{:S(2)}, u32[]{:S(2)}) collective-permute-start(f32[3,2,2,32,128]{4,3,2,1,0:T(8,128)S(1)} %get-tuple-element.26), channel_id=1, source_target_pairs={{0,2},{2,0},{4,6},{6,4},{8,10},{10,8},{12,14},{14,12},{16,18},{18,... | collective-permute-start | bytes 589832 | tf_op jit(solution)/shard_map/ppermute | solution.py:430
  24.8 12.9 %collective-permute-start.2 = (f32[3,2,2,32,128]{4,3,2,1,0:T(8,128)S(1)}, f32[3,2,2,32,128]{4,3,2,1,0:T(8,128)S(1)}, u32[]{:S(2)}, u32[]{:S(2)}) collective-permute-start(f32[3,2,2,32,128]{4,3,2,1,0:T(8,128)S(1)} %get-tuple-element.27), channel_id=1, source_target_pairs={{2,4},{4,2},{6,8},{8,6},{10,12},{12,10},{14,16},{16,14},{18,20},{2... | collective-permute-start | bytes 589832 | tf_op jit(solution)/shard_map/ppermute | solution.py:430
  32.4 11.1 %collective-permute-start.13 = (f32[18,16,128]{2,1,0:T(8,128)S(1)}, f32[18,16,128]{2,1,0:T(8,128)S(1)}, u32[]{:S(2)}, u32[]{:S(2)}) collective-permute-start(f32[18,16,128]{2,1,0:T(8,128)S(1)} %get-tuple-element.37.refs_0_), channel_id=1, source_target_pairs={{0,1},{1,0},{2,3},{3,2},{4,5},{5,4},{6,7},{7,6},{8,9},{9,8},{10,11... | collective-permute-start | bytes 442376 | tf_op jit(solution)/shard_map/ppermute | solution.py:541
  32.4 6.4 %collective-permute-start.5 = (f32[3,2,16,128]{3,2,1,0:T(8,128)S(1)}, f32[3,2,16,128]{3,2,1,0:T(8,128)S(1)}, u32[]{:S(2)}, u32[]{:S(2)}) collective-permute-start(f32[3,2,16,128]{3,2,1,0:T(8,128)S(1)} %get-tuple-element.33), channel_id=1, source_target_pairs={{0,2},{2,0},{4,6},{6,4},{8,10},{10,8},{12,14},{14,12},{16,18},{18,... | collective-permute-start | bytes 147464 | tf_op jit(solution)/shard_map/ppermute | solution.py:430
  35.0 7.8 %collective-permute-start.6 = (f32[3,2,16,128]{3,2,1,0:T(8,128)S(1)}, f32[3,2,16,128]{3,2,1,0:T(8,128)S(1)}, u32[]{:S(2)}, u32[]{:S(2)}) collective-permute-start(f32[3,2,16,128]{3,2,1,0:T(8,128)S(1)} %get-tuple-element.34), channel_id=1, source_target_pairs={{2,4},{4,2},{6,8},{8,6},{10,12},{12,10},{14,16},{16,14},{18,20},{2... | collective-permute-start | bytes 147464 | tf_op jit(solution)/shard_map/ppermute | solution.py:430
where the time goes:
time: 44.9 us; the launch traced here: 44.7 us
  starting transfers between devices  22.9 us (51%)
  waiting for transfers between devices  13.6 us (30%)
  Pallas kernels  7.41 us (17%)
  between operations  0.79 us (2%)
    ppermute x12, starting transfers between devices, wide_swap(): lax.ppermute(value, 'wide', [(i, partner(i)) for i in range(count) if 0 <...  22.8 us
    ppermute x12, waiting for transfers between devices, wide_swap(): lax.ppermute(value, 'wide', [(i, partner(i)) for i in range(count) if 0 <...  13.3 us
    pallas_call x1, Pallas kernels, per_device(): pl.pallas_call(x_one, out_shape=(jax.ShapeDtypeStruct(padded, F32),) + tu...  2.54 us
    pallas_call x1, Pallas kernels, per_device(): call(lambda *refs: xy_deep(*refs, pair=count_y == 2, own3=own3), [(7, own...  1.28 us
    pallas_call x1, Pallas kernels, per_device(): detail_one, = call(z_one, [(7, m, own, cl * LANES)], [])(d, rde, rdo, h)  1.17 us
    pallas_call x1, Pallas kernels, per_device(): call(lambda *refs: xy_one(*refs, one_halo=count_y == 2), [padded, (nz, cl...  1.11 us
  transfers between devices with their start and end apart: 14, of which 9 were waited for; matrix products, arithmetic and copies ran while one was open for 0% of the time, Pallas kernels for 10%

commit v1 on v0

--- a/solution.py
+++ b/solution.py
@@ -229,7 +229,7 @@
                 do_ref[b, j, c] = jnp.where(even, left[j], right[j])
 
 
-def xy_two(ll_ref, re_ref, ro_ref, th_ref, tl_ref, g_ref, d2_ref, h_ref, pe_ref, po_ref, lw, ys):
+def xy_two(ll_ref, re_ref, ro_ref, th_ref, tl_ref, t3h_ref, t3l_ref, g_ref, d2_ref, h_ref, pe_ref, po_ref, lw, ys):
     nz, cl, tall, _ = ll_ref.shape
     own = tall - SUB
     m = nz // 2
@@ -257,11 +257,13 @@
         def rows(xb):
             return lambda t: ys[i, xb, pl.ds(SUB + t, half, stride=2), :]
 
-        g_ref[i] = taps_low(rows(0))
-        d2_ref[0, i] = taps_low(rows(1))
-        d2_ref[1, i] = taps_high(rows(0))
-        d2_ref[2, i] = taps_high(rows(1))
-    for b in range(3):
+        d2_ref[0, i] = taps_low(rows(0))
+        d2_ref[1, i] = taps_low(rows(1))
+        d2_ref[2, i] = taps_high(rows(0))
+        d2_ref[3, i] = taps_high(rows(1))
+    deeper = dot3(halves(d2_ref[0].reshape(m * half, LANES)), t3h_ref[...], t3l_ref[...])
+    g_ref[...] = deeper.reshape(m, half, LANES)
+    for b in range(4):
         s = [d2_ref[b, 2 * i] for i in range(m // 2)]
         d = [d2_ref[b, 2 * i + 1] for i in range(m // 2)]
         right, left = z_right(s, d), z_left(s, d)
@@ -296,15 +298,33 @@
                 one_ref[4 + b, i, :, lanes] = high[i]
 
 
-def z_two(d_ref, re_ref, ro_ref, h_ref, two_ref):
+def z_two(d_ref, re_ref, ro_ref, two_ref):
     m = d_ref.shape[1] // 2
-    for i in range(m):
-        two_ref[3, i] = h_ref[i]
-    for b in range(3):
+    for b in range(4):
         low, high = halo_lift(lambda k: d_ref[b, k], m, lambda j: re_ref[b, j], lambda j: ro_ref[b, j])
         for i in range(m):
-            two_ref[b, i] = low[i]
-            two_ref[4 + b, i] = high[i]
+            if b:
+                two_ref[b - 1, i] = low[i]
+            two_ref[3 + b, i] = high[i]
+
+
+def near_slot(z, above):
+    return jnp.where((lax.rem(z, 2) == 0) == above, 4, 12)
+
+
+def pack_last(own_ref, four_ref, eight_ref, twelve_ref, px_ref, py_ref):
+    me = lax.axis_index("wide")
+    z = me // 4
+    lanes = lax.broadcasted_iota(jnp.int32, own_ref.shape, 2)
+    half = LANES // 2
+    for out_ref, bit in ((px_ref, 1), (py_ref, 2)):
+        above = lax.rem(me // bit, 2) == 0
+        close = near_slot(z, above) == 4
+        out_ref[0] = own_ref[...]
+        out_ref[1] = jnp.where(close, four_ref[...], twelve_ref[...])
+        rest = jnp.where(close, twelve_ref[...], four_ref[...])
+        for i in range(own_ref.shape[0]):
+            out_ref[2, i] = jnp.where(lanes[i] < half, rest[i], pltpu.roll(eight_ref[i], half, 1))
 
 
 def mirrored(j, size):
@@ -315,14 +335,29 @@
 
 def z_deep(*refs, slots):
     got_refs = refs[: len(slots)]
-    h2_ref, zz_ref, seq, low2, low3 = refs[len(slots) :]
-    m = got_refs[0].shape[-3]
+    t4h_ref, t4l_ref, zz_ref, seq, low2, low3 = refs[len(slots) :]
+    m, half = got_refs[0].shape[-3], zz_ref.shape[1]
     me = lax.axis_index("wide")
+
+    def put(offset, piece):
+        seq[pl.ds(lax.bitwise_xor(me, offset) * m, m)] = piece
+
     for ref, offsets in zip(got_refs, slots):
+        if isinstance(offsets, int):
+            partner = lax.bitwise_xor(me, offsets)
+            above = lax.rem(partner // (1 if offsets == 1 else 2), 2) == 0
+            slot = near_slot(me // 4, above)
+            keep = lax.broadcasted_iota(jnp.int32, (half, LANES), 1) < LANES // 2
+            put(offsets, ref[0])
+            put(lax.bitwise_xor(slot, offsets), ref[1])
+            for k, offset in ((0, lax.bitwise_xor(16 - slot, offsets)), (1, offsets ^ 8)):
+                chip = lax.bitwise_xor(me, offset)
+                for i in range(m):
+                    value = pltpu.roll(ref[2, i], LANES // 2, 1) if k else ref[2, i]
+                    seq[chip * m + i] = jnp.where(keep, value, 0.0)
+            continue
         for k, offset in enumerate(offsets):
-            chip = lax.bitwise_xor(me, offset)
-            piece = ref[k] if len(ref.shape) == 4 else ref[...]
-            seq[pl.ds(chip * m, m)] = piece
+            put(offset, ref[k] if len(ref.shape) == 4 else ref[...])
     size = seq.shape[0]
 
     def at_of(ref, size, i):
@@ -330,8 +365,6 @@
 
     for i in range(size // 2):
         low2[i] = taps_low(at_of(seq, size, i))
-    for i in range(m // 2):
-        h2_ref[i] = taps_high(at_of(seq, size, me * (m // 2) + i))
     size2 = size // 2
     for i in range(size2 // 2):
         low3[i] = taps_low(at_of(low2, size2, i))
@@ -341,8 +374,11 @@
         zz_ref[i] = low3[me * own3 + i]
         zz_ref[own3 + i] = taps_high(at_of(low2, size2, me * own3 + i))
     for i in range(size3 // 2):
-        zz_ref[2 * own3 + i] = taps_low(at_of(low3, size3, i))
-        zz_ref[2 * own3 + size3 // 2 + i] = taps_high(at_of(low3, size3, i))
+        seq[i] = taps_low(at_of(low3, size3, i))
+        seq[size3 // 2 + i] = taps_high(at_of(low3, size3, i))
+    rows = size3 * half
+    got = dot3(halves(seq[:size3].reshape(rows, LANES)), t4h_ref[...], t4l_ref[...])
+    zz_ref[2 * own3 :] = got.reshape(size3, half, LANES)
 
 
 def pick(me, value, count):
@@ -358,19 +394,14 @@
         zz_ref, other_ref = refs[:2]
     else:
         zz_ref = refs[0]
-    th3, tl3, th4, tl4, three_ref, four_ref, xs, ys = refs[2 if pair else 1 :]
+    three_ref, four_ref, xs, ys = refs[2 if pair else 1 :]
     me = lax.axis_index("narrow")
     count = lax.axis_size("narrow")
     planes, rows = zz_ref.shape[-3], zz_ref.shape[-2]
     full = rows * count
 
     def put(value, start):
-        a = 2 * own3
-        got = dot3(halves(value[:a].reshape(a * rows, LANES)), th3[...], tl3[...])
-        xs[:a, pl.ds(start, rows), :] = got.reshape(a, rows, LANES)
-        b = planes - a
-        got = dot3(halves(value[a:].reshape(b * rows, LANES)), th4[...], tl4[...])
-        xs[a:, pl.ds(start, rows), :] = got.reshape(b, rows, LANES)
+        xs[:, pl.ds(start, rows), :] = value
 
     if pair:
         put(zz_ref[...], pl.multiple_of(SUB + rows * me, SUB))
@@ -503,21 +534,28 @@
         xy_two,
         [
             (m, half, LANES),
-            (3, m, half, LANES),
+            (4, m, half, LANES),
             (m, cl, own, LANES),
-            (3, 2, half, LANES),
-            (3, 2, half, LANES),
+            (4, 2, half, LANES),
+            (4, 2, half, LANES),
         ],
         [(m, own + SUB, cl * LANES), (m, 2, own + 2 * SUB, LANES)],
-    )(ll, re, ro, *np_split(lift_table(nx // 2)))
+    )(ll, re, ro, *np_split(lift_table(nx // 2)), *np_split(lift_table(nx // 4)))
     pieces, slots = [g], [[0]]
     stages = gather_stages(count_z)
     for n, masks in enumerate(stages):
+        final = n == len(stages) - 1
+        if final and count_z == 16:
+            block = (3, m, half, LANES)
+            px, py = call(pack_last, [block, block], [])(*pieces)
+            for mask in masks:
+                pieces.append(wide_swap(px if mask == 1 else py, xor_pair(mask)))
+                slots.append(mask)
+            break
+        whole, flat = g, [0]
         if n:
             whole = jnp.concatenate([p.reshape((-1, m, half, LANES)) for p in pieces], 0)
             flat = [o for part in slots for o in part]
-        else:
-            whole, flat = g, [0]
         pieces = [whole]
         for mask in masks:
             pieces.append(wide_swap(whole, xor_pair(mask)))
@@ -527,16 +565,15 @@
     size = m * count_z
     own3 = m // 4
     planes = 2 * own3 + size // 4
-    h2, zz = call(
+    table4 = np.zeros((LANES, LANES))
+    table4[: nx // 8, : nx // 8] = lift_table(nx // 8)
+    (zz,) = call(
         lambda *refs: z_deep(*refs, slots=slots),
-        [(m // 2, half, LANES), (planes, half, LANES)],
+        [(planes, half, LANES)],
         [(size, half, LANES), (size // 2, half, LANES), (size // 4, half, LANES)],
-    )(*pieces)
+    )(*pieces, *np_split(table4))
     (detail_one,) = call(z_one, [(7, m, own, cl * LANES)], [])(d, rde, rdo, h)
-    (detail_two,) = call(z_two, [(7, m // 2, half, LANES)], [])(d2, re2, ro2, h2)
-    table3 = lift_table(nx // 4)
-    table4 = table3[:, : nx // 8] @ lift_table(nx // 8)
-    table4 = np.concatenate([table4, np.zeros((nx // 4, LANES - nx // 8))], 1)
+    (detail_two,) = call(z_two, [(7, m // 2, half, LANES)], [])(d2, re2, ro2)
     if count_y == 2:
         rest = (zz, lax.ppermute(zz, "narrow", [(0, 1), (1, 0)]))
     else:
@@ -546,7 +583,7 @@
         lambda *refs: xy_deep(*refs, pair=count_y == 2, own3=own3),
         [(7, own3, half // 2, nx // 8), (8, size // 8, half // 4, nx // 16)],
         [(planes, full + 2 * SUB, LANES), (planes - 2 * own3, full // 2 + 2 * SUB, LANES)],
-    )(*rest, *np_split(table3), *np_split(table4))
+    )(*rest)
     return detail_one, detail_two, detail_three, bands_four
 
 

time: 44.9 us -> 45.1 us (level)
  the two profiles are of different devices: /device:TPU:14 before, /device:TPU:6 now
where the time goes in v1:
time: 45.1 us; the launch traced here: 45 us
  starting transfers between devices  21.3 us (47%)
  waiting for transfers between devices  15.2 us (34%)
  Pallas kernels  7.65 us (17%)
  between operations  0.76 us (2%)
    ppermute x12, starting transfers between devices, wide_swap(): lax.ppermute(value, 'wide', [(i, partner(i)) for i in range(count) if 0 <...  21.2 us
    ppermute x12, waiting for transfers between devices, wide_swap(): lax.ppermute(value, 'wide', [(i, partner(i)) for i in range(count) if 0 <...  14.9 us
    pallas_call x1, Pallas kernels, per_device(): pl.pallas_call(x_one, out_shape=(jax.ShapeDtypeStruct(padded, F32),) + tu...  2.54 us
    pallas_call x1, Pallas kernels, per_device(): detail_one, = call(z_one, [(7, m, own, cl * LANES)], [])(d, rde, rdo, h)  1.17 us
    pallas_call x1, Pallas kernels, per_device(): call(lambda *refs: xy_one(*refs, one_halo=count_y == 2), [padded, (nz, cl...  1.11 us
    pallas_call x1, Pallas kernels, per_device(): call(lambda *refs: xy_deep(*refs, pair=count_y == 2, own3=own3), [(7, own...  1.08 us
  transfers between devices with their start and end apart: 14, of which 9 were waited for; matrix products, arithmetic and copies ran while one was open for 0% of the time, Pallas kernels for 11%

profile of v1, /device:TPU:6, one launch (start us, length us, event | category | flops | bytes accessed | tf_op | source)
XLA Modules:
  0.0 45.0 jit_solution(7864170017443995479)
XLA Ops:
  0.6 0.1 collective-permute-start
  0.7 2.5 %x_one.1 = (f32[8,4,112,128]{3,2,1,0:T(8,128)S(1)}, bf16[512,512]{1,0:T(8,128)(2,1)S(1)}, bf16[512,512]{1,0:T(8,128)(2,1)S(1)}) custom-call(f32[8,64,512]{2,1,0:T(8,128)} %x_hbm.1, bf16[512,512]{1,0:T(8,128)(2,1)} %constant.16.clone.th_hbm, bf16[512,512]{1,0:T(8,128)(2,1)} %constant.17.clone.tl_hbm), custom_call_target="tpu_custom_call" | custom-call | flops 2000000 | bytes 2000000 | tf_op jit(solution)/shard_map/x_one/pallas_call | solution.py:503
  3.3 0.3 collective-permute-done.refs_1_
  3.6 0.0 copy-start
  3.6 0.0 copy-start.1
  3.6 0.0 copy-start.4
  3.6 0.0 copy-start.5
  3.6 0.0 copy-start.2
  3.6 0.0 copy-start.3
  3.6 1.1 %shard_map.120 = (f32[8,4,112,128]{3,2,1,0:T(8,128)S(1)}, f32[8,2,40,128]{3,2,1,0:T(8,128)S(1)}, f32[3,8,2,32,128]{4,3,2,1,0:T(8,128)S(1)}, f32[2,2,40,128]{3,2,...) custom-call(f32[8,4,112,128]{3,2,1,0:T(8,128)S(1)} %get-tuple-elemen, ...), custom_call_target="tpu_custom_call", output_to_operand_aliasing={{0}: (0, {})} | custom-call | flops 2000000 | bytes 2000000 | tf_op jit(solution)/shard_map/pallas_call | solution.py:514
  4.7 0.6 %collective-permute-start.3 = (f32[2,2,40,128]{3,2,1,0:T(8,128)S(1)}, f32[2,2,40,128]{3,2,1,0:T(8,128)S(1)}, u32[]{:S(2)}, u32[]{:S(2)}) collective-permute-start(f32[2,2,40,128]{3,2,1,0:T(8,128)S(1)} %get-tuple-element.29), channel_id=1, source_target_pairs={{0,2},{2,0},{4,6},{6,4},{8,10},{10,8},{12,14},{14,12},{16,18},{18,... | collective-permute-start | bytes 245768 | tf_op jit(solution)/shard_map/ppermute | solution.py:461
  5.3 4.3 %collective-permute-start.4 = (f32[2,2,40,128]{3,2,1,0:T(8,128)S(1)}, f32[2,2,40,128]{3,2,1,0:T(8,128)S(1)}, u32[]{:S(2)}, u32[]{:S(2)}) collective-permute-start(f32[2,2,40,128]{3,2,1,0:T(8,128)S(1)} %get-tuple-element.30), channel_id=1, source_target_pairs={{2,4},{4,2},{6,8},{8,6},{10,12},{12,10},{14,16},{16,14},{18,20},{2... | collective-permute-start | bytes 245768 | tf_op jit(solution)/shard_map/ppermute | solution.py:461
  9.7 0.0 collective-permute-done.3.re_ref
  9.7 3.8 %collective-permute-done.4.ro_ref = f32[2,2,40,128]{3,2,1,0:T(8,128)S(1)} collective-permute-done((f32[2,2,40,128]{3,2,1,0:T(8,128)S(1)}, f32[2,2,40,128]{3,2,1,0:T(8,128)S(1)}, u32[]{:S(2)}, u32[]{:S(2)}) %collective-permute-start.4) | collective-permute-done | bytes 81952 | tf_op jit(solution)/shard_map/ppermute | solution.py:461
  13.4 0.0 copy-done
  13.5 0.0 copy-done.1
  13.5 0.0 copy-done.4
  13.5 0.0 copy-done.5
  13.5 0.5 %shard_map.121 = (f32[4,16,128]{2,1,0:T(8,128)S(1)}, f32[4,4,16,128]{3,2,1,0:T(8,128)S(1)}, f32[4,2,32,128]{3,2,1,0:T(8,128)S(1)}, f32[4,2,16,128]{3,2,1,0:T(8,128)S(1)}, f32[4,2,16,128]{3,2,1,0:T(8,128)S(1)}) custom-call(f32[8,2,40,128]{3,2,1,0:T(8,128)S(1)} %get-tuple-element.28.ll_ref, f32[2,2,40,128]{3,2,1,0:T(8,128)S(1)} %collective-permute-done.3.re_ref, ...), custom_call_target="tpu_custom_call" | custom-call | flops 2000000 | bytes 2000000 | tf_op jit(solution)/shard_map/pallas_call | solution.py:533
  13.9 0.0 collective-permute-start.9
  13.9 3.1 %collective-permute-start.8 = (f32[4,16,128]{2,1,0:T(8,128)S(1)}, f32[4,16,128]{2,1,0:T(8,128)S(1)}, u32[]{:S(2)}, u32[]{:S(2)}) collective-permute-start(f32[4,16,128]{2,1,0:T(8,128)S(1)} %get-tuple-element.35.own_ref.refs_0_), channel_id=1, source_target_pairs={{0,16},{2,18},{4,20},{6,22},{8,24},{10,26},{12,28},{14,30},{16,0},... | collective-permute-start | bytes 98312 | tf_op jit(solution)/shard_map/ppermute | solution.py:461
  17.0 1.3 %collective-permute-start.7 = (f32[4,16,128]{2,1,0:T(8,128)S(1)}, f32[4,16,128]{2,1,0:T(8,128)S(1)}, u32[]{:S(2)}, u32[]{:S(2)}) collective-permute-start(f32[4,16,128]{2,1,0:T(8,128)S(1)} %get-tuple-element.35.own_ref.refs_0_), channel_id=1, source_target_pairs={{0,8},{2,10},{4,12},{6,14},{8,0},{10,2},{12,4},{14,6},{16,24},{18,... | collective-permute-start | bytes 98312 | tf_op jit(solution)/shard_map/ppermute | solution.py:461
  18.3 1.3 %collective-permute-done.9.twelve_ref.refs_3_ = f32[4,16,128]{2,1,0:T(8,128)S(1)} collective-permute-done((f32[4,16,128]{2,1,0:T(8,128)S(1)}, f32[4,16,128]{2,1,0:T(8,128)S(1)}, u32[]{:S(2)}, u32[]{:S(2)}) %collective-permute-start.9) | collective-permute-done | bytes 32800 | tf_op jit(solution)/shard_map/ppermute | solution.py:461
  19.7 0.3 collective-permute-done.8.eight_ref.refs_2_
  19.9 1.0 %collective-permute-done.7.four_ref.refs_1_ = f32[4,16,128]{2,1,0:T(8,128)S(1)} collective-permute-done((f32[4,16,128]{2,1,0:T(8,128)S(1)}, f32[4,16,128]{2,1,0:T(8,128)S(1)}, u32[]{:S(2)}, u32[]{:S(2)}) %collective-permute-start.7) | collective-permute-done | bytes 32800 | tf_op jit(solution)/shard_map/ppermute | solution.py:461
  20.9 0.1 shard_map.124
  21.0 2.1 %collective-permute-start.10 = (f32[3,4,16,128]{3,2,1,0:T(8,128)S(1)}, f32[3,4,16,128]{3,2,1,0:T(8,128)S(1)}, u32[]{:S(2)}, u32[]{:S(2)}) collective-permute-start(f32[3,4,16,128]{3,2,1,0:T(8,128)S(1)} %get-tuple-element.36), channel_id=1, source_target_pairs={{0,2},{2,0},{4,6},{6,4},{8,10},{10,8},{12,14},{14,12},{16,18},{18,... | collective-permute-start | bytes 294920 | tf_op jit(solution)/shard_map/ppermute | solution.py:461
  23.1 0.9 %collective-permute-start.12 = (f32[3,4,16,128]{3,2,1,0:T(8,128)S(1)}, f32[3,4,16,128]{3,2,1,0:T(8,128)S(1)}, u32[]{:S(2)}, u32[]{:S(2)}) collective-permute-start(f32[3,4,16,128]{3,2,1,0:T(8,128)S(1)} %get-tuple-element.37), channel_id=1, source_target_pairs={{0,6},{2,4},{4,2},{6,0},{8,14},{10,12},{12,10},{14,8},{16,22},{18,... | collective-permute-start | bytes 294920 | tf_op jit(solution)/shard_map/ppermute | solution.py:461
  24.0 0.6 %collective-permute-start.11 = (f32[3,4,16,128]{3,2,1,0:T(8,128)S(1)}, f32[3,4,16,128]{3,2,1,0:T(8,128)S(1)}, u32[]{:S(2)}, u32[]{:S(2)}) collective-permute-start(f32[3,4,16,128]{3,2,1,0:T(8,128)S(1)} %get-tuple-element.37), channel_id=1, source_target_pairs={{0,4},{2,6},{4,0},{6,2},{8,12},{10,14},{12,8},{14,10},{16,20},{18,... | collective-permute-start | bytes 294920 | tf_op jit(solution)/shard_map/ppermute | solution.py:461
  24.7 1.9 %collective-permute-start.1 = (f32[3,2,2,32,128]{4,3,2,1,0:T(8,128)S(1)}, f32[3,2,2,32,128]{4,3,2,1,0:T(8,128)S(1)}, u32[]{:S(2)}, u32[]{:S(2)}) collective-permute-start(f32[3,2,2,32,128]{4,3,2,1,0:T(8,128)S(1)} %get-tuple-element.26), channel_id=1, source_target_pairs={{0,2},{2,0},{4,6},{6,4},{8,10},{10,8},{12,14},{14,12},{16,18},{18,... | collective-permute-start | bytes 589832 | tf_op jit(solution)/shard_map/ppermute | solution.py:461
  26.6 2.1 %collective-permute-start.2 = (f32[3,2,2,32,128]{4,3,2,1,0:T(8,128)S(1)}, f32[3,2,2,32,128]{4,3,2,1,0:T(8,128)S(1)}, u32[]{:S(2)}, u32[]{:S(2)}) collective-permute-start(f32[3,2,2,32,128]{4,3,2,1,0:T(8,128)S(1)} %get-tuple-element.27), channel_id=1, source_target_pairs={{2,4},{4,2},{6,8},{8,6},{10,12},{12,10},{14,16},{16,14},{18,20},{2... | collective-permute-start | bytes 589832 | tf_op jit(solution)/shard_map/ppermute | solution.py:461
  28.7 0.0 collective-permute-done.10.refs_4_
  28.7 0.5 %collective-permute-done.12.refs_6_ = f32[3,4,16,128]{3,2,1,0:T(8,128)S(1)} collective-permute-done((f32[3,4,16,128]{3,2,1,0:T(8,128)S(1)}, f32[3,4,16,128]{3,2,1,0:T(8,128)S(1)}, u32[]{:S(2)}, u32[]{:S(2)}) %collective-permute-start.12) | collective-permute-done | bytes 98336 | tf_op jit(solution)/shard_map/ppermute | solution.py:461
  29.2 2.6 %collective-permute-done.11.refs_5_ = f32[3,4,16,128]{3,2,1,0:T(8,128)S(1)} collective-permute-done((f32[3,4,16,128]{3,2,1,0:T(8,128)S(1)}, f32[3,4,16,128]{3,2,1,0:T(8,128)S(1)}, u32[]{:S(2)}, u32[]{:S(2)}) %collective-permute-start.11) | collective-permute-done | bytes 98336 | tf_op jit(solution)/shard_map/ppermute | solution.py:461
  31.8 0.0 copy-done.2
  31.8 0.0 copy-done.3
  31.8 0.5 %shard_map.125.refs_0_ = f32[18,16,128]{2,1,0:T(8,128)S(1)} custom-call(f32[4,16,128]{2,1,0:T(8,128)S(1)} %get-tuple-element.35.own_ref.refs_0_, f32[4,16,128]{2,1,0:T(8,128)S(1)} %collective-permute-done.7.four_ref.refs_1_, f32[4,16,128]{2,1,0:T(8,128)S(1)} %collective-permute-done.8.eight_ref.refs_2_, ...), custom_call_target="tpu_custom_call" | custom-call | flops 2000000 | bytes 2000000 | tf_op jit(solution)/shard_map/pallas_call | solution.py:570
  32.3 0.1 collective-permute-start.13
  32.4 1.6 %collective-permute-start.5 = (f32[4,2,16,128]{3,2,1,0:T(8,128)S(1)}, f32[4,2,16,128]{3,2,1,0:T(8,128)S(1)}, u32[]{:S(2)}, u32[]{:S(2)}) collective-permute-start(f32[4,2,16,128]{3,2,1,0:T(8,128)S(1)} %get-tuple-element.33), channel_id=1, source_target_pairs={{0,2},{2,0},{4,6},{6,4},{8,10},{10,8},{12,14},{14,12},{16,18},{18,... | collective-permute-start | bytes 196616 | tf_op jit(solution)/shard_map/ppermute | solution.py:461
  34.0 2.5 %collective-permute-start.6 = (f32[4,2,16,128]{3,2,1,0:T(8,128)S(1)}, f32[4,2,16,128]{3,2,1,0:T(8,128)S(1)}, u32[]{:S(2)}, u32[]{:S(2)}) collective-permute-start(f32[4,2,16,128]{3,2,1,0:T(8,128)S(1)} %get-tuple-element.34), channel_id=1, source_target_pairs={{2,4},{4,2},{6,8},{8,6},{10,12},{12,10},{14,16},{16,14},{18,20},{2... | collective-permute-start | bytes 196616 | tf_op jit(solution)/shard_map/ppermute | solution.py:461
  36.5 0.3 collective-permute-done.5.re_ref
  36.9 5.1 %collective-permute-done.6.ro_ref = f32[4,2,16,128]{3,2,1,0:T(8,128)S(1)} collective-permute-done((f32[4,2,16,128]{3,2,1,0:T(8,128)S(1)}, f32[4,2,16,128]{3,2,1,0:T(8,128)S(1)}, u32[]{:S(2)}, u32[]{:S(2)}) %collective-permute-start.6) | collective-permute-done | bytes 65568 | tf_op jit(solution)/shard_map/ppermute | solution.py:461
  42.0 0.7 %shard_map.123 = f32[7,2,16,128]{3,2,1,0:T(8,128)} custom-call(f32[4,4,16,128]{3,2,1,0:T(8,128)S(1)} %get-tuple-element.32.d_ref, f32[4,2,16,128]{3,2,1,0:T(8,128)S(1)} %collective-permute-done.5.re_ref, f32[4,2,16,128]{3,2,1,0:T(8,128)S(1)} %collective-permute-done.6.ro_ref), custom_call_target="tpu_custom_call" | custom-call | flops 2000000 | bytes 2000000 | tf_op jit(solution)/shard_map/pallas_call | solution.py:576
  42.7 0.0 collective-permute-done.1.re_ref
  42.7 0.0 collective-permute-done.2.ro_ref
  42.7 1.2 %shard_map.122 = f32[7,4,32,256]{3,2,1,0:T(8,128)} custom-call(f32[3,8,2,32,128]{4,3,2,1,0:T(8,128)S(1)} %get-tuple-element.25.d_ref, f32[3,2,2,32,128]{4,3,2,1,0:T(8,128)S(1)} %collective-permute-done.1.re_ref, f32[3,2,2,32,128]{4,3,2,1,0:T(8,128)S(1)} %collective-permute-done.2.ro_ref, f32[4,2,32,128]{3,2,1,0:T(8,128)S(1)} %get-tuple-element.31.h_ref), custom_call_target="tpu_custom_call" | custom-call | flops 2000000 | bytes 2000000 | tf_op jit(solution)/shard_map/pallas_call | solution.py:575
  43.9 0.0 collective-permute-done.13.refs_1_
  43.9 1.1 %shard_map.126 = (f32[7,1,8,64]{3,2,1,0:T(8,128)}, f32[8,8,4,32]{3,2,1,0:T(4,128)}) custom-call(f32[18,16,128]{2,1,0:T(8,128)S(1)} %shard_map.125.refs_0_, f32[18,16,128]{2,1,0:T(8,128)S(1)} %collective-permute-done.13.refs_1_), custom_call_target="tpu_custom_call" | custom-call | flops 2000000 | bytes 2000000 | tf_op jit(solution)/shard_map/pallas_call | solution.py:582
Async XLA Ops:
  0.6 2.9 %collective-permute-start = (f32[8,64,512]{2,1,0:T(8,128)}, f32[8,64,512]{2,1,0:T(8,128)S(1)}, u32[]{:S(2)}, u32[]{:S(2)}) collective-permute-start(f32[8,64,512]{2,1,0:T(8,128)} %x_hbm.1), channel_id=1, source_target_pairs={{0,1},{1,0},{2,3},{3,2},{4,5},{5,4},{6,7},{7,6},{8,9},{9,8},{10,11... | collective-permute-start | bytes 3145736 | tf_op jit(solution)/shard_map/ppermute | solution.py:493
  3.6 9.9 %copy-start = (bf16[256,256]{1,0:T(8,128)(2,1)S(1)}, bf16[256,256]{1,0:T(8,128)(2,1)}, u32[]{:S(2)}) copy-start(bf16[256,256]{1,0:T(8,128)(2,1)} %constant.19.clone.tl_ref) | copy-start | bytes 393220
  3.6 9.9 %copy-start.1 = (bf16[256,256]{1,0:T(8,128)(2,1)S(1)}, bf16[256,256]{1,0:T(8,128)(2,1)}, u32[]{:S(2)}) copy-start(bf16[256,256]{1,0:T(8,128)(2,1)} %constant.18.clone.th_ref) | copy-start | bytes 393220
  3.6 9.9 %copy-start.4 = (bf16[128,128]{1,0:T(8,128)(2,1)S(1)}, bf16[128,128]{1,0:T(8,128)(2,1)}, u32[]{:S(2)}) copy-start(bf16[128,128]{1,0:T(8,128)(2,1)} %constant.21.clone.t3l_ref) | copy-start | bytes 98308
  3.6 9.9 %copy-start.5 = (bf16[128,128]{1,0:T(8,128)(2,1)S(1)}, bf16[128,128]{1,0:T(8,128)(2,1)}, u32[]{:S(2)}) copy-start(bf16[128,128]{1,0:T(8,128)(2,1)} %constant.20.clone.t3h_ref) | copy-start | bytes 98308
  3.6 28.2 %copy-start.2 = (bf16[128,128]{1,0:T(8,128)(2,1)S(1)}, bf16[128,128]{1,0:T(8,128)(2,1)}, u32[]{:S(2)}) copy-start(bf16[128,128]{1,0:T(8,128)(2,1)} %constant.23.clone.refs_8_) | copy-start | bytes 98308
  3.6 28.2 %copy-start.3 = (bf16[128,128]{1,0:T(8,128)(2,1)S(1)}, bf16[128,128]{1,0:T(8,128)(2,1)}, u32[]{:S(2)}) copy-start(bf16[128,128]{1,0:T(8,128)(2,1)} %constant.22.clone.refs_7_) | copy-start | bytes 98308
  4.7 5.0 %collective-permute-start.3 = (f32[2,2,40,128]{3,2,1,0:T(8,128)S(1)}, f32[2,2,40,128]{3,2,1,0:T(8,128)S(1)}, u32[]{:S(2)}, u32[]{:S(2)}) collective-permute-start(f32[2,2,40,128]{3,2,1,0:T(8,128)S(1)} %get-tuple-element.29), channel_id=1, source_target_pairs={{0,2},{2,0},{4,6},{6,4},{8,10},{10,8},{12,14},{14,12},{16,18},{18,... | collective-permute-start | bytes 245768 | tf_op jit(solution)/shard_map/ppermute | solution.py:461
  5.3 8.1 %collective-permute-start.4 = (f32[2,2,40,128]{3,2,1,0:T(8,128)S(1)}, f32[2,2,40,128]{3,2,1,0:T(8,128)S(1)}, u32[]{:S(2)}, u32[]{:S(2)}) collective-permute-start(f32[2,2,40,128]{3,2,1,0:T(8,128)S(1)} %get-tuple-element.30), channel_id=1, source_target_pairs={{2,4},{4,2},{6,8},{8,6},{10,12},{12,10},{14,16},{16,14},{18,20},{2... | collective-permute-start | bytes 245768 | tf_op jit(solution)/shard_map/ppermute | solution.py:461
  13.9 5.7 %collective-permute-start.9 = (f32[4,16,128]{2,1,0:T(8,128)S(1)}, f32[4,16,128]{2,1,0:T(8,128)S(1)}, u32[]{:S(2)}, u32[]{:S(2)}) collective-permute-start(f32[4,16,128]{2,1,0:T(8,128)S(1)} %get-tuple-element.35.own_ref.refs_0_), channel_id=1, source_target_pairs={{0,24},{2,26},{4,28},{6,30},{8,16},{10,18},{12,20},{14,22},{16,8},... | collective-permute-start | bytes 98312 | tf_op jit(solution)/shard_map/ppermute | solution.py:461
  13.9 6.0 %collective-permute-start.8 = (f32[4,16,128]{2,1,0:T(8,128)S(1)}, f32[4,16,128]{2,1,0:T(8,128)S(1)}, u32[]{:S(2)}, u32[]{:S(2)}) collective-permute-start(f32[4,16,128]{2,1,0:T(8,128)S(1)} %get-tuple-element.35.own_ref.refs_0_), channel_id=1, source_target_pairs={{0,16},{2,18},{4,20},{6,22},{8,24},{10,26},{12,28},{14,30},{16,0},... | collective-permute-start | bytes 98312 | tf_op jit(solution)/shard_map/ppermute | solution.py:461
  17.0 3.9 %collective-permute-start.7 = (f32[4,16,128]{2,1,0:T(8,128)S(1)}, f32[4,16,128]{2,1,0:T(8,128)S(1)}, u32[]{:S(2)}, u32[]{:S(2)}) collective-permute-start(f32[4,16,128]{2,1,0:T(8,128)S(1)} %get-tuple-element.35.own_ref.refs_0_), channel_id=1, source_target_pairs={{0,8},{2,10},{4,12},{6,14},{8,0},{10,2},{12,4},{14,6},{16,24},{18,... | collective-permute-start | bytes 98312 | tf_op jit(solution)/shard_map/ppermute | solution.py:461
  21.0 7.7 %collective-permute-start.10 = (f32[3,4,16,128]{3,2,1,0:T(8,128)S(1)}, f32[3,4,16,128]{3,2,1,0:T(8,128)S(1)}, u32[]{:S(2)}, u32[]{:S(2)}) collective-permute-start(f32[3,4,16,128]{3,2,1,0:T(8,128)S(1)} %get-tuple-element.36), channel_id=1, source_target_pairs={{0,2},{2,0},{4,6},{6,4},{8,10},{10,8},{12,14},{14,12},{16,18},{18,... | collective-permute-start | bytes 294920 | tf_op jit(solution)/shard_map/ppermute | solution.py:461
  23.1 6.1 %collective-permute-start.12 = (f32[3,4,16,128]{3,2,1,0:T(8,128)S(1)}, f32[3,4,16,128]{3,2,1,0:T(8,128)S(1)}, u32[]{:S(2)}, u32[]{:S(2)}) collective-permute-start(f32[3,4,16,128]{3,2,1,0:T(8,128)S(1)} %get-tuple-element.37), channel_id=1, source_target_pairs={{0,6},{2,4},{4,2},{6,0},{8,14},{10,12},{12,10},{14,8},{16,22},{18,... | collective-permute-start | bytes 294920 | tf_op jit(solution)/shard_map/ppermute | solution.py:461
  24.0 7.8 %collective-permute-start.11 = (f32[3,4,16,128]{3,2,1,0:T(8,128)S(1)}, f32[3,4,16,128]{3,2,1,0:T(8,128)S(1)}, u32[]{:S(2)}, u32[]{:S(2)}) collective-permute-start(f32[3,4,16,128]{3,2,1,0:T(8,128)S(1)} %get-tuple-element.37), channel_id=1, source_target_pairs={{0,4},{2,6},{4,0},{6,2},{8,12},{10,14},{12,8},{14,10},{16,20},{18,... | collective-permute-start | bytes 294920 | tf_op jit(solution)/shard_map/ppermute | solution.py:461
  24.7 18.0 %collective-permute-start.1 = (f32[3,2,2,32,128]{4,3,2,1,0:T(8,128)S(1)}, f32[3,2,2,32,128]{4,3,2,1,0:T(8,128)S(1)}, u32[]{:S(2)}, u32[]{:S(2)}) collective-permute-start(f32[3,2,2,32,128]{4,3,2,1,0:T(8,128)S(1)} %get-tuple-element.26), channel_id=1, source_target_pairs={{0,2},{2,0},{4,6},{6,4},{8,10},{10,8},{12,14},{14,12},{16,18},{18,... | collective-permute-start | bytes 589832 | tf_op jit(solution)/shard_map/ppermute | solution.py:461
  26.6 16.1 %collective-permute-start.2 = (f32[3,2,2,32,128]{4,3,2,1,0:T(8,128)S(1)}, f32[3,2,2,32,128]{4,3,2,1,0:T(8,128)S(1)}, u32[]{:S(2)}, u32[]{:S(2)}) collective-permute-start(f32[3,2,2,32,128]{4,3,2,1,0:T(8,128)S(1)} %get-tuple-element.27), channel_id=1, source_target_pairs={{2,4},{4,2},{6,8},{8,6},{10,12},{12,10},{14,16},{16,14},{18,20},{2... | collective-permute-start | bytes 589832 | tf_op jit(solution)/shard_map/ppermute | solution.py:461
  32.3 11.6 %collective-permute-start.13 = (f32[18,16,128]{2,1,0:T(8,128)S(1)}, f32[18,16,128]{2,1,0:T(8,128)S(1)}, u32[]{:S(2)}, u32[]{:S(2)}) collective-permute-start(f32[18,16,128]{2,1,0:T(8,128)S(1)} %shard_map.125.refs_0_), channel_id=1, source_target_pairs={{0,1},{1,0},{2,3},{3,2},{4,5},{5,4},{6,7},{7,6},{8,9},{9,8},{10,11... | collective-permute-start | bytes 442376 | tf_op jit(solution)/shard_map/ppermute | solution.py:578
  32.4 4.5 %collective-permute-start.5 = (f32[4,2,16,128]{3,2,1,0:T(8,128)S(1)}, f32[4,2,16,128]{3,2,1,0:T(8,128)S(1)}, u32[]{:S(2)}, u32[]{:S(2)}) collective-permute-start(f32[4,2,16,128]{3,2,1,0:T(8,128)S(1)} %get-tuple-element.33), channel_id=1, source_target_pairs={{0,2},{2,0},{4,6},{6,4},{8,10},{10,8},{12,14},{14,12},{16,18},{18,... | collective-permute-start | bytes 196616 | tf_op jit(solution)/shard_map/ppermute | solution.py:461
  34.0 7.9 %collective-permute-start.6 = (f32[4,2,16,128]{3,2,1,0:T(8,128)S(1)}, f32[4,2,16,128]{3,2,1,0:T(8,128)S(1)}, u32[]{:S(2)}, u32[]{:S(2)}) collective-permute-start(f32[4,2,16,128]{3,2,1,0:T(8,128)S(1)} %get-tuple-element.34), channel_id=1, source_target_pairs={{2,4},{4,2},{6,8},{8,6},{10,12},{12,10},{14,16},{16,14},{18,20},{2... | collective-permute-start | bytes 196616 | tf_op jit(solution)/shard_map/ppermute | solution.py:461

commit v2 on v1

--- a/solution.py
+++ b/solution.py
@@ -457,8 +457,13 @@
 
 
 def wide_swap(value, partner):
-    count = lax.axis_size("wide")
-    return lax.ppermute(value, "wide", [(i, partner(i)) for i in range(count) if 0 <= partner(i) < count])
+    count, cores = lax.axis_size("wide"), lax.axis_size("narrow")
+    pairs = []
+    for i in range(count):
+        for k in range(cores):
+            j, c = (partner(i), k) if 0 <= partner(i) < count else (i, k ^ 1)
+            pairs.append((i * cores + k, j * cores + c))
+    return lax.ppermute(value, ("wide", "narrow"), pairs)
 
 
 def even_pair(i):

time: 45.1 us -> 43.2 us (0.958)
  the two profiles are of different devices: /device:TPU:6 before, /device:TPU:2 now
where the time goes in v2:
time: 43.2 us; the launch traced here: 43.1 us
  starting transfers between devices  19.4 us (45%)
  waiting for transfers between devices  15.3 us (35%)
  Pallas kernels  7.66 us (18%)
  between operations  0.74 us (2%)
    ppermute x12, starting transfers between devices, wide_swap(): return lax.ppermute(value, ('wide', 'narrow'), pairs)  19.3 us
    ppermute x12, waiting for transfers between devices, wide_swap(): return lax.ppermute(value, ('wide', 'narrow'), pairs)  15 us
    pallas_call x1, Pallas kernels, per_device(): pl.pallas_call(x_one, out_shape=(jax.ShapeDtypeStruct(padded, F32),) + tu...  2.54 us
    pallas_call x1, Pallas kernels, per_device(): detail_one, = call(z_one, [(7, m, own, cl * LANES)], [])(d, rde, rdo, h)  1.17 us
    pallas_call x1, Pallas kernels, per_device(): call(lambda *refs: xy_one(*refs, one_halo=count_y == 2), [padded, (nz, cl...  1.12 us
    pallas_call x1, Pallas kernels, per_device(): call(lambda *refs: xy_deep(*refs, pair=count_y == 2, own3=own3), [(7, own...  1.08 us
  transfers between devices with their start and end apart: 14, of which 7 were waited for; matrix products, arithmetic and copies ran while one was open for 0% of the time, Pallas kernels for 11%

profile of v2, /device:TPU:2, one launch (start us, length us, event | category | flops | bytes accessed | tf_op | source)
XLA Modules:
  0.0 43.1 jit_solution(8694679968442192581)
XLA Ops:
  0.6 0.1 collective-permute-start
  0.7 2.5 %x_one.1 = (f32[8,4,112,128]{3,2,1,0:T(8,128)S(1)}, bf16[512,512]{1,0:T(8,128)(2,1)S(1)}, bf16[512,512]{1,0:T(8,128)(2,1)S(1)}) custom-call(f32[8,64,512]{2,1,0:T(8,128)} %x_hbm.1, bf16[512,512]{1,0:T(8,128)(2,1)} %constant.16.clone.th_hbm, bf16[512,512]{1,0:T(8,128)(2,1)} %constant.17.clone.tl_hbm), custom_call_target="tpu_custom_call" | custom-call | flops 2000000 | bytes 2000000 | tf_op jit(solution)/shard_map/x_one/pallas_call | solution.py:508
  3.3 0.3 collective-permute-done.refs_1_
  3.6 0.0 copy-start
  3.6 0.0 copy-start.1
  3.6 0.0 copy-start.4
  3.6 0.0 copy-start.5
  3.6 0.0 copy-start.2
  3.6 0.0 copy-start.3
  3.6 1.1 %shard_map.120 = (f32[8,4,112,128]{3,2,1,0:T(8,128)S(1)}, f32[8,2,40,128]{3,2,1,0:T(8,128)S(1)}, f32[3,8,2,32,128]{4,3,2,1,0:T(8,128)S(1)}, f32[2,2,40,128]{3,2,...) custom-call(f32[8,4,112,128]{3,2,1,0:T(8,128)S(1)} %get-tuple-elemen, ...), custom_call_target="tpu_custom_call", output_to_operand_aliasing={{0}: (0, {})} | custom-call | flops 2000000 | bytes 2000000 | tf_op jit(solution)/shard_map/pallas_call | solution.py:519
  4.7 0.1 collective-permute-start.3
  4.8 3.0 %collective-permute-start.4 = (f32[2,2,40,128]{3,2,1,0:T(8,128)S(1)}, f32[2,2,40,128]{3,2,1,0:T(8,128)S(1)}, u32[]{:S(2)}, u32[]{:S(2)}) collective-permute-start(f32[2,2,40,128]{3,2,1,0:T(8,128)S(1)} %get-tuple-element.30), channel_id=1, source_target_pairs={{0,1},{1,0},{2,4},{3,5},{4,2},{5,3},{6,8},{7,9},{8,6},{9,7},{10,12... | collective-permute-start | bytes 245768 | tf_op jit(solution)/shard_map/ppermute | solution.py:466
  7.8 1.6 %collective-permute-done.3.re_ref = f32[2,2,40,128]{3,2,1,0:T(8,128)S(1)} collective-permute-done((f32[2,2,40,128]{3,2,1,0:T(8,128)S(1)}, f32[2,2,40,128]{3,2,1,0:T(8,128)S(1)}, u32[]{:S(2)}, u32[]{:S(2)}) %collective-permute-start.3) | collective-permute-done | bytes 81952 | tf_op jit(solution)/shard_map/ppermute | solution.py:466
  9.4 2.7 %collective-permute-done.4.ro_ref = f32[2,2,40,128]{3,2,1,0:T(8,128)S(1)} collective-permute-done((f32[2,2,40,128]{3,2,1,0:T(8,128)S(1)}, f32[2,2,40,128]{3,2,1,0:T(8,128)S(1)}, u32[]{:S(2)}, u32[]{:S(2)}) %collective-permute-start.4) | collective-permute-done | bytes 81952 | tf_op jit(solution)/shard_map/ppermute | solution.py:466
  12.1 0.0 copy-done
  12.1 0.0 copy-done.1
  12.1 0.0 copy-done.4
  12.1 0.0 copy-done.5
  12.1 0.5 %shard_map.121 = (f32[4,16,128]{2,1,0:T(8,128)S(1)}, f32[4,4,16,128]{3,2,1,0:T(8,128)S(1)}, f32[4,2,32,128]{3,2,1,0:T(8,128)S(1)}, f32[4,2,16,128]{3,2,1,0:T(8,128)S(1)}, f32[4,2,16,128]{3,2,1,0:T(8,128)S(1)}) custom-call(f32[8,2,40,128]{3,2,1,0:T(8,128)S(1)} %get-tuple-element.28.ll_ref, f32[2,2,40,128]{3,2,1,0:T(8,128)S(1)} %collective-permute-done.3.re_ref, ...), custom_call_target="tpu_custom_call" | custom-call | flops 2000000 | bytes 2000000 | tf_op jit(solution)/shard_map/pallas_call | solution.py:538
  12.6 3.6 %collective-permute-start.9 = (f32[4,16,128]{2,1,0:T(8,128)S(1)}, f32[4,16,128]{2,1,0:T(8,128)S(1)}, u32[]{:S(2)}, u32[]{:S(2)}) collective-permute-start(f32[4,16,128]{2,1,0:T(8,128)S(1)} %get-tuple-element.35.own_ref.refs_0_), channel_id=1, source_target_pairs={{0,24},{1,25},{2,26},{3,27},{4,28},{5,29},{6,30},{7,31},{8,16},{9,... | collective-permute-start | bytes 98312 | tf_op jit(solution)/shard_map/ppermute | solution.py:466
  16.2 0.0 collective-permute-start.8
  16.2 0.8 %collective-permute-start.7 = (f32[4,16,128]{2,1,0:T(8,128)S(1)}, f32[4,16,128]{2,1,0:T(8,128)S(1)}, u32[]{:S(2)}, u32[]{:S(2)}) collective-permute-start(f32[4,16,128]{2,1,0:T(8,128)S(1)} %get-tuple-element.35.own_ref.refs_0_), channel_id=1, source_target_pairs={{0,8},{1,9},{2,10},{3,11},{4,12},{5,13},{6,14},{7,15},{8,0},{9,1},... | collective-permute-start | bytes 98312 | tf_op jit(solution)/shard_map/ppermute | solution.py:466
  17.0 1.6 %collective-permute-done.9.twelve_ref.refs_3_ = f32[4,16,128]{2,1,0:T(8,128)S(1)} collective-permute-done((f32[4,16,128]{2,1,0:T(8,128)S(1)}, f32[4,16,128]{2,1,0:T(8,128)S(1)}, u32[]{:S(2)}, u32[]{:S(2)}) %collective-permute-start.9) | collective-permute-done | bytes 32800 | tf_op jit(solution)/shard_map/ppermute | solution.py:466
  18.5 2.5 %collective-permute-done.8.eight_ref.refs_2_ = f32[4,16,128]{2,1,0:T(8,128)S(1)} collective-permute-done((f32[4,16,128]{2,1,0:T(8,128)S(1)}, f32[4,16,128]{2,1,0:T(8,128)S(1)}, u32[]{:S(2)}, u32[]{:S(2)}) %collective-permute-start.8) | collective-permute-done | bytes 32800 | tf_op jit(solution)/shard_map/ppermute | solution.py:466
  21.0 0.0 collective-permute-done.7.four_ref.refs_1_
  21.0 0.1 shard_map.124
  21.1 1.1 %collective-permute-start.10 = (f32[3,4,16,128]{3,2,1,0:T(8,128)S(1)}, f32[3,4,16,128]{3,2,1,0:T(8,128)S(1)}, u32[]{:S(2)}, u32[]{:S(2)}) collective-permute-start(f32[3,4,16,128]{3,2,1,0:T(8,128)S(1)} %get-tuple-element.36), channel_id=1, source_target_pairs={{0,2},{1,3},{2,0},{3,1},{4,6},{5,7},{6,4},{7,5},{8,10},{9,11},{10,... | collective-permute-start | bytes 294920 | tf_op jit(solution)/shard_map/ppermute | solution.py:466
  22.1 0.4 collective-permute-start.12
  22.5 2.1 %collective-permute-start.11 = (f32[3,4,16,128]{3,2,1,0:T(8,128)S(1)}, f32[3,4,16,128]{3,2,1,0:T(8,128)S(1)}, u32[]{:S(2)}, u32[]{:S(2)}) collective-permute-start(f32[3,4,16,128]{3,2,1,0:T(8,128)S(1)} %get-tuple-element.37), channel_id=1, source_target_pairs={{0,4},{1,5},{2,6},{3,7},{4,0},{5,1},{6,2},{7,3},{8,12},{9,13},{10,... | collective-permute-start | bytes 294920 | tf_op jit(solution)/shard_map/ppermute | solution.py:466
  24.6 1.0 %collective-permute-start.1 = (f32[3,2,2,32,128]{4,3,2,1,0:T(8,128)S(1)}, f32[3,2,2,32,128]{4,3,2,1,0:T(8,128)S(1)}, u32[]{:S(2)}, u32[]{:S(2)}) collective-permute-start(f32[3,2,2,32,128]{4,3,2,1,0:T(8,128)S(1)} %get-tuple-element.26), channel_id=1, source_target_pairs={{0,2},{1,3},{2,0},{3,1},{4,6},{5,7},{6,4},{7,5},{8,10},{9,11},{10,... | collective-permute-start | bytes 589832 | tf_op jit(solution)/shard_map/ppermute | solution.py:466
  25.6 0.5 %collective-permute-start.2 = (f32[3,2,2,32,128]{4,3,2,1,0:T(8,128)S(1)}, f32[3,2,2,32,128]{4,3,2,1,0:T(8,128)S(1)}, u32[]{:S(2)}, u32[]{:S(2)}) collective-permute-start(f32[3,2,2,32,128]{4,3,2,1,0:T(8,128)S(1)} %get-tuple-element.27), channel_id=1, source_target_pairs={{0,1},{1,0},{2,4},{3,5},{4,2},{5,3},{6,8},{7,9},{8,6},{9,7},{10,12... | collective-permute-start | bytes 589832 | tf_op jit(solution)/shard_map/ppermute | solution.py:466
  26.1 2.8 %collective-permute-done.10.refs_4_ = f32[3,4,16,128]{3,2,1,0:T(8,128)S(1)} collective-permute-done((f32[3,4,16,128]{3,2,1,0:T(8,128)S(1)}, f32[3,4,16,128]{3,2,1,0:T(8,128)S(1)}, u32[]{:S(2)}, u32[]{:S(2)}) %collective-permute-start.10) | collective-permute-done | bytes 98336 | tf_op jit(solution)/shard_map/ppermute | solution.py:466
  28.9 0.0 collective-permute-done.12.refs_6_
  28.9 0.0 collective-permute-done.11.refs_5_
  28.9 0.0 copy-done.2
  28.9 0.0 copy-done.3
  28.9 0.5 %shard_map.125.refs_0_ = f32[18,16,128]{2,1,0:T(8,128)S(1)} custom-call(f32[4,16,128]{2,1,0:T(8,128)S(1)} %get-tuple-element.35.own_ref.refs_0_, f32[4,16,128]{2,1,0:T(8,128)S(1)} %collective-permute-done.7.four_ref.refs_1_, f32[4,16,128]{2,1,0:T(8,128)S(1)} %collective-permute-done.8.eight_ref.refs_2_, ...), custom_call_target="tpu_custom_call" | custom-call | flops 2000000 | bytes 2000000 | tf_op jit(solution)/shard_map/pallas_call | solution.py:575
  29.4 0.1 collective-permute-start.13
  29.5 3.4 %collective-permute-start.5 = (f32[4,2,16,128]{3,2,1,0:T(8,128)S(1)}, f32[4,2,16,128]{3,2,1,0:T(8,128)S(1)}, u32[]{:S(2)}, u32[]{:S(2)}) collective-permute-start(f32[4,2,16,128]{3,2,1,0:T(8,128)S(1)} %get-tuple-element.33), channel_id=1, source_target_pairs={{0,2},{1,3},{2,0},{3,1},{4,6},{5,7},{6,4},{7,5},{8,10},{9,11},{10,... | collective-permute-start | bytes 196616 | tf_op jit(solution)/shard_map/ppermute | solution.py:466
  33.0 3.4 %collective-permute-start.6 = (f32[4,2,16,128]{3,2,1,0:T(8,128)S(1)}, f32[4,2,16,128]{3,2,1,0:T(8,128)S(1)}, u32[]{:S(2)}, u32[]{:S(2)}) collective-permute-start(f32[4,2,16,128]{3,2,1,0:T(8,128)S(1)} %get-tuple-element.34), channel_id=1, source_target_pairs={{0,1},{1,0},{2,4},{3,5},{4,2},{5,3},{6,8},{7,9},{8,6},{9,7},{10,12... | collective-permute-start | bytes 196616 | tf_op jit(solution)/shard_map/ppermute | solution.py:466
  36.3 0.0 collective-permute-done.5.re_ref
  36.3 3.8 %collective-permute-done.6.ro_ref = f32[4,2,16,128]{3,2,1,0:T(8,128)S(1)} collective-permute-done((f32[4,2,16,128]{3,2,1,0:T(8,128)S(1)}, f32[4,2,16,128]{3,2,1,0:T(8,128)S(1)}, u32[]{:S(2)}, u32[]{:S(2)}) %collective-permute-start.6) | collective-permute-done | bytes 65568 | tf_op jit(solution)/shard_map/ppermute | solution.py:466
  40.1 0.7 %shard_map.123 = f32[7,2,16,128]{3,2,1,0:T(8,128)} custom-call(f32[4,4,16,128]{3,2,1,0:T(8,128)S(1)} %get-tuple-element.32.d_ref, f32[4,2,16,128]{3,2,1,0:T(8,128)S(1)} %collective-permute-done.5.re_ref, f32[4,2,16,128]{3,2,1,0:T(8,128)S(1)} %collective-permute-done.6.ro_ref), custom_call_target="tpu_custom_call" | custom-call | flops 2000000 | bytes 2000000 | tf_op jit(solution)/shard_map/pallas_call | solution.py:581
  40.8 0.0 collective-permute-done.1.re_ref
  40.8 0.0 collective-permute-done.2.ro_ref
  40.8 1.2 %shard_map.122 = f32[7,4,32,256]{3,2,1,0:T(8,128)} custom-call(f32[3,8,2,32,128]{4,3,2,1,0:T(8,128)S(1)} %get-tuple-element.25.d_ref, f32[3,2,2,32,128]{4,3,2,1,0:T(8,128)S(1)} %collective-permute-done.1.re_ref, f32[3,2,2,32,128]{4,3,2,1,0:T(8,128)S(1)} %collective-permute-done.2.ro_ref, f32[4,2,32,128]{3,2,1,0:T(8,128)S(1)} %get-tuple-element.31.h_ref), custom_call_target="tpu_custom_call" | custom-call | flops 2000000 | bytes 2000000 | tf_op jit(solution)/shard_map/pallas_call | solution.py:580
  42.0 0.0 collective-permute-done.13.refs_1_
  42.0 1.1 %shard_map.126 = (f32[7,1,8,64]{3,2,1,0:T(8,128)}, f32[8,8,4,32]{3,2,1,0:T(4,128)}) custom-call(f32[18,16,128]{2,1,0:T(8,128)S(1)} %shard_map.125.refs_0_, f32[18,16,128]{2,1,0:T(8,128)S(1)} %collective-permute-done.13.refs_1_), custom_call_target="tpu_custom_call" | custom-call | flops 2000000 | bytes 2000000 | tf_op jit(solution)/shard_map/pallas_call | solution.py:587
Async XLA Ops:
  0.6 2.9 %collective-permute-start = (f32[8,64,512]{2,1,0:T(8,128)}, f32[8,64,512]{2,1,0:T(8,128)S(1)}, u32[]{:S(2)}, u32[]{:S(2)}) collective-permute-start(f32[8,64,512]{2,1,0:T(8,128)} %x_hbm.1), channel_id=1, source_target_pairs={{0,1},{1,0},{2,3},{3,2},{4,5},{5,4},{6,7},{7,6},{8,9},{9,8},{10,11... | collective-permute-start | bytes 3145736 | tf_op jit(solution)/shard_map/ppermute | solution.py:498
  3.6 8.5 %copy-start = (bf16[256,256]{1,0:T(8,128)(2,1)S(1)}, bf16[256,256]{1,0:T(8,128)(2,1)}, u32[]{:S(2)}) copy-start(bf16[256,256]{1,0:T(8,128)(2,1)} %constant.19.clone.tl_ref) | copy-start | bytes 393220
  3.6 8.5 %copy-start.1 = (bf16[256,256]{1,0:T(8,128)(2,1)S(1)}, bf16[256,256]{1,0:T(8,128)(2,1)}, u32[]{:S(2)}) copy-start(bf16[256,256]{1,0:T(8,128)(2,1)} %constant.18.clone.th_ref) | copy-start | bytes 393220
  3.6 8.5 %copy-start.4 = (bf16[128,128]{1,0:T(8,128)(2,1)S(1)}, bf16[128,128]{1,0:T(8,128)(2,1)}, u32[]{:S(2)}) copy-start(bf16[128,128]{1,0:T(8,128)(2,1)} %constant.21.clone.t3l_ref) | copy-start | bytes 98308
  3.6 8.5 %copy-start.5 = (bf16[128,128]{1,0:T(8,128)(2,1)S(1)}, bf16[128,128]{1,0:T(8,128)(2,1)}, u32[]{:S(2)}) copy-start(bf16[128,128]{1,0:T(8,128)(2,1)} %constant.20.clone.t3h_ref) | copy-start | bytes 98308
  3.6 25.4 %copy-start.2 = (bf16[128,128]{1,0:T(8,128)(2,1)S(1)}, bf16[128,128]{1,0:T(8,128)(2,1)}, u32[]{:S(2)}) copy-start(bf16[128,128]{1,0:T(8,128)(2,1)} %constant.23.clone.refs_8_) | copy-start | bytes 98308
  3.6 25.4 %copy-start.3 = (bf16[128,128]{1,0:T(8,128)(2,1)S(1)}, bf16[128,128]{1,0:T(8,128)(2,1)}, u32[]{:S(2)}) copy-start(bf16[128,128]{1,0:T(8,128)(2,1)} %constant.22.clone.refs_7_) | copy-start | bytes 98308
  4.7 4.6 %collective-permute-start.3 = (f32[2,2,40,128]{3,2,1,0:T(8,128)S(1)}, f32[2,2,40,128]{3,2,1,0:T(8,128)S(1)}, u32[]{:S(2)}, u32[]{:S(2)}) collective-permute-start(f32[2,2,40,128]{3,2,1,0:T(8,128)S(1)} %get-tuple-element.29), channel_id=1, source_target_pairs={{0,2},{1,3},{2,0},{3,1},{4,6},{5,7},{6,4},{7,5},{8,10},{9,11},{10,... | collective-permute-start | bytes 245768 | tf_op jit(solution)/shard_map/ppermute | solution.py:466
  4.8 7.3 %collective-permute-start.4 = (f32[2,2,40,128]{3,2,1,0:T(8,128)S(1)}, f32[2,2,40,128]{3,2,1,0:T(8,128)S(1)}, u32[]{:S(2)}, u32[]{:S(2)}) collective-permute-start(f32[2,2,40,128]{3,2,1,0:T(8,128)S(1)} %get-tuple-element.30), channel_id=1, source_target_pairs={{0,1},{1,0},{2,4},{3,5},{4,2},{5,3},{6,8},{7,9},{8,6},{9,7},{10,12... | collective-permute-start | bytes 245768 | tf_op jit(solution)/shard_map/ppermute | solution.py:466
  12.6 6.0 %collective-permute-start.9 = (f32[4,16,128]{2,1,0:T(8,128)S(1)}, f32[4,16,128]{2,1,0:T(8,128)S(1)}, u32[]{:S(2)}, u32[]{:S(2)}) collective-permute-start(f32[4,16,128]{2,1,0:T(8,128)S(1)} %get-tuple-element.35.own_ref.refs_0_), channel_id=1, source_target_pairs={{0,24},{1,25},{2,26},{3,27},{4,28},{5,29},{6,30},{7,31},{8,16},{9,... | collective-permute-start | bytes 98312 | tf_op jit(solution)/shard_map/ppermute | solution.py:466
  16.2 4.8 %collective-permute-start.8 = (f32[4,16,128]{2,1,0:T(8,128)S(1)}, f32[4,16,128]{2,1,0:T(8,128)S(1)}, u32[]{:S(2)}, u32[]{:S(2)}) collective-permute-start(f32[4,16,128]{2,1,0:T(8,128)S(1)} %get-tuple-element.35.own_ref.refs_0_), channel_id=1, source_target_pairs={{0,16},{1,17},{2,18},{3,19},{4,20},{5,21},{6,22},{7,23},{8,24},{9,... | collective-permute-start | bytes 98312 | tf_op jit(solution)/shard_map/ppermute | solution.py:466
  16.2 4.8 %collective-permute-start.7 = (f32[4,16,128]{2,1,0:T(8,128)S(1)}, f32[4,16,128]{2,1,0:T(8,128)S(1)}, u32[]{:S(2)}, u32[]{:S(2)}) collective-permute-start(f32[4,16,128]{2,1,0:T(8,128)S(1)} %get-tuple-element.35.own_ref.refs_0_), channel_id=1, source_target_pairs={{0,8},{1,9},{2,10},{3,11},{4,12},{5,13},{6,14},{7,15},{8,0},{9,1},... | collective-permute-start | bytes 98312 | tf_op jit(solution)/shard_map/ppermute | solution.py:466
  21.1 7.8 %collective-permute-start.10 = (f32[3,4,16,128]{3,2,1,0:T(8,128)S(1)}, f32[3,4,16,128]{3,2,1,0:T(8,128)S(1)}, u32[]{:S(2)}, u32[]{:S(2)}) collective-permute-start(f32[3,4,16,128]{3,2,1,0:T(8,128)S(1)} %get-tuple-element.36), channel_id=1, source_target_pairs={{0,2},{1,3},{2,0},{3,1},{4,6},{5,7},{6,4},{7,5},{8,10},{9,11},{10,... | collective-permute-start | bytes 294920 | tf_op jit(solution)/shard_map/ppermute | solution.py:466
  22.1 6.8 %collective-permute-start.12 = (f32[3,4,16,128]{3,2,1,0:T(8,128)S(1)}, f32[3,4,16,128]{3,2,1,0:T(8,128)S(1)}, u32[]{:S(2)}, u32[]{:S(2)}) collective-permute-start(f32[3,4,16,128]{3,2,1,0:T(8,128)S(1)} %get-tuple-element.37), channel_id=1, source_target_pairs={{0,6},{1,7},{2,4},{3,5},{4,2},{5,3},{6,0},{7,1},{8,14},{9,15},{10,... | collective-permute-start | bytes 294920 | tf_op jit(solution)/shard_map/ppermute | solution.py:466
  22.5 6.4 %collective-permute-start.11 = (f32[3,4,16,128]{3,2,1,0:T(8,128)S(1)}, f32[3,4,16,128]{3,2,1,0:T(8,128)S(1)}, u32[]{:S(2)}, u32[]{:S(2)}) collective-permute-start(f32[3,4,16,128]{3,2,1,0:T(8,128)S(1)} %get-tuple-element.37), channel_id=1, source_target_pairs={{0,4},{1,5},{2,6},{3,7},{4,0},{5,1},{6,2},{7,3},{8,12},{9,13},{10,... | collective-permute-start | bytes 294920 | tf_op jit(solution)/shard_map/ppermute | solution.py:466
  24.6 16.2 %collective-permute-start.1 = (f32[3,2,2,32,128]{4,3,2,1,0:T(8,128)S(1)}, f32[3,2,2,32,128]{4,3,2,1,0:T(8,128)S(1)}, u32[]{:S(2)}, u32[]{:S(2)}) collective-permute-start(f32[3,2,2,32,128]{4,3,2,1,0:T(8,128)S(1)} %get-tuple-element.26), channel_id=1, source_target_pairs={{0,2},{1,3},{2,0},{3,1},{4,6},{5,7},{6,4},{7,5},{8,10},{9,11},{10,... | collective-permute-start | bytes 589832 | tf_op jit(solution)/shard_map/ppermute | solution.py:466
  25.6 15.2 %collective-permute-start.2 = (f32[3,2,2,32,128]{4,3,2,1,0:T(8,128)S(1)}, f32[3,2,2,32,128]{4,3,2,1,0:T(8,128)S(1)}, u32[]{:S(2)}, u32[]{:S(2)}) collective-permute-start(f32[3,2,2,32,128]{4,3,2,1,0:T(8,128)S(1)} %get-tuple-element.27), channel_id=1, source_target_pairs={{0,1},{1,0},{2,4},{3,5},{4,2},{5,3},{6,8},{7,9},{8,6},{9,7},{10,12... | collective-permute-start | bytes 589832 | tf_op jit(solution)/shard_map/ppermute | solution.py:466
  29.4 12.6 %collective-permute-start.13 = (f32[18,16,128]{2,1,0:T(8,128)S(1)}, f32[18,16,128]{2,1,0:T(8,128)S(1)}, u32[]{:S(2)}, u32[]{:S(2)}) collective-permute-start(f32[18,16,128]{2,1,0:T(8,128)S(1)} %shard_map.125.refs_0_), channel_id=1, source_target_pairs={{0,1},{1,0},{2,3},{3,2},{4,5},{5,4},{6,7},{7,6},{8,9},{9,8},{10,11... | collective-permute-start | bytes 442376 | tf_op jit(solution)/shard_map/ppermute | solution.py:583
  29.5 6.8 %collective-permute-start.5 = (f32[4,2,16,128]{3,2,1,0:T(8,128)S(1)}, f32[4,2,16,128]{3,2,1,0:T(8,128)S(1)}, u32[]{:S(2)}, u32[]{:S(2)}) collective-permute-start(f32[4,2,16,128]{3,2,1,0:T(8,128)S(1)} %get-tuple-element.33), channel_id=1, source_target_pairs={{0,2},{1,3},{2,0},{3,1},{4,6},{5,7},{6,4},{7,5},{8,10},{9,11},{10,... | collective-permute-start | bytes 196616 | tf_op jit(solution)/shard_map/ppermute | solution.py:466
  33.0 7.2 %collective-permute-start.6 = (f32[4,2,16,128]{3,2,1,0:T(8,128)S(1)}, f32[4,2,16,128]{3,2,1,0:T(8,128)S(1)}, u32[]{:S(2)}, u32[]{:S(2)}) collective-permute-start(f32[4,2,16,128]{3,2,1,0:T(8,128)S(1)} %get-tuple-element.34), channel_id=1, source_target_pairs={{0,1},{1,0},{2,4},{3,5},{4,2},{5,3},{6,8},{7,9},{8,6},{9,7},{10,12... | collective-permute-start | bytes 196616 | tf_op jit(solution)/shard_map/ppermute | solution.py:466

commit v3 on v2

--- a/solution.py
+++ b/solution.py
@@ -17,7 +17,7 @@
 LANES = 128
 SUB = 8
 HALO = 16
-PARTS = 2
+PARTS = 1
 EDGE = 4
 BASE = 24
 F32 = jnp.float32
@@ -85,6 +85,11 @@
     return (HIGH[0] * at(1) + HIGH[1] * (at(0) + at(2))) + (
         HIGH[2] * (at(-1) + at(3)) + HIGH[3] * (at(-2) + at(4))
     )
+
+
+def taps_both(at):
+    rows = {t: at(t) for t in range(-4, 5)}
+    return taps_low(rows.__getitem__), taps_high(rows.__getitem__)
 
 
 def z_right(s, d):
@@ -198,13 +203,11 @@
             def rows(chunk, start, n):
                 return lambda t: xs[p, chunk, pl.ds(start + t, n, stride=2), :]
 
-            ll_ref[p, c, :own, :] = taps_low(rows(c, BASE, own))
+            ll_ref[p, c, :own, :], d_ref[1, p, c] = taps_both(rows(c, BASE, own))
             below = taps_low(rows(c, BASE + ny, SUB))
             above = taps_low(rows(c, BASE - 2 * SUB, SUB))
             ll_ref[p, c, own : own + SUB, :] = jnp.where(upper, below, above)
-            d_ref[0, p, c] = taps_low(rows(cl + c, BASE, own))
-            d_ref[1, p, c] = taps_high(rows(c, BASE, own))
-            d_ref[2, p, c] = taps_high(rows(cl + c, BASE, own))
+            d_ref[0, p, c], d_ref[2, p, c] = taps_both(rows(cl + c, BASE, own))
 
     @pl.when(last)
     def _():

time: 43.2 us -> 43.2 us (level)
  no operation moved by 1% of the time
where the time goes in v3:
time: 43.2 us; the launch traced here: 43.1 us
  starting transfers between devices  19.4 us (45%)
  waiting for transfers between devices  15.3 us (35%)
  Pallas kernels  7.64 us (18%)
  between operations  0.74 us (2%)
    ppermute x12, starting transfers between devices, wide_swap(): return lax.ppermute(value, ('wide', 'narrow'), pairs)  19.2 us
    ppermute x12, waiting for transfers between devices, wide_swap(): return lax.ppermute(value, ('wide', 'narrow'), pairs)  14.9 us
    pallas_call x1, Pallas kernels, per_device(): pl.pallas_call(x_one, out_shape=(jax.ShapeDtypeStruct(padded, F32),) + tu...  2.52 us
    pallas_call x1, Pallas kernels, per_device(): detail_one, = call(z_one, [(7, m, own, cl * LANES)], [])(d, rde, rdo, h)  1.17 us
    pallas_call x1, Pallas kernels, per_device(): call(lambda *refs: xy_one(*refs, one_halo=count_y == 2), [padded, (nz, cl...  1.12 us
    pallas_call x1, Pallas kernels, per_device(): call(lambda *refs: xy_deep(*refs, pair=count_y == 2, own3=own3), [(7, own...  1.08 us
  transfers between devices with their start and end apart: 14, of which 7 were waited for; matrix products, arithmetic and copies ran while one was open for 0% of the time, Pallas kernels for 11%

profile of v3, /device:TPU:2, one launch (start us, length us, event | category | flops | bytes accessed | tf_op | source)
XLA Modules:
  0.0 43.1 jit_solution(216998263573548528)
XLA Ops:
  0.6 0.1 collective-permute-start
  0.7 2.5 %x_one.1 = (f32[8,4,112,128]{3,2,1,0:T(8,128)S(1)}, bf16[512,512]{1,0:T(8,128)(2,1)S(1)}, bf16[512,512]{1,0:T(8,128)(2,1)S(1)}) custom-call(f32[8,64,512]{2,1,0:T(8,128)} %x_hbm.1, bf16[512,512]{1,0:T(8,128)(2,1)} %constant.16.clone.th_hbm, bf16[512,512]{1,0:T(8,128)(2,1)} %constant.17.clone.tl_hbm), custom_call_target="tpu_custom_call" | custom-call | flops 2000000 | bytes 2000000 | tf_op jit(solution)/shard_map/x_one/pallas_call | solution.py:511
  3.2 0.3 collective-permute-done.refs_1_
  3.6 0.0 copy-start
  3.6 0.0 copy-start.1
  3.6 0.0 copy-start.4
  3.6 0.0 copy-start.5
  3.6 0.0 copy-start.2
  3.6 0.0 copy-start.3
  3.6 1.1 %shard_map.120 = (f32[8,4,112,128]{3,2,1,0:T(8,128)S(1)}, f32[8,2,40,128]{3,2,1,0:T(8,128)S(1)}, f32[3,8,2,32,128]{4,3,2,1,0:T(8,128)S(1)}, f32[2,2,40,128]{3,2,...) custom-call(f32[8,4,112,128]{3,2,1,0:T(8,128)S(1)} %get-tuple-elemen, ...), custom_call_target="tpu_custom_call", output_to_operand_aliasing={{0}: (0, {})} | custom-call | flops 2000000 | bytes 2000000 | tf_op jit(solution)/shard_map/pallas_call | solution.py:522
  4.7 0.1 collective-permute-start.3
  4.8 3.0 %collective-permute-start.4 = (f32[2,2,40,128]{3,2,1,0:T(8,128)S(1)}, f32[2,2,40,128]{3,2,1,0:T(8,128)S(1)}, u32[]{:S(2)}, u32[]{:S(2)}) collective-permute-start(f32[2,2,40,128]{3,2,1,0:T(8,128)S(1)} %get-tuple-element.30), channel_id=1, source_target_pairs={{0,1},{1,0},{2,4},{3,5},{4,2},{5,3},{6,8},{7,9},{8,6},{9,7},{10,12... | collective-permute-start | bytes 245768 | tf_op jit(solution)/shard_map/ppermute | solution.py:469
  7.8 1.6 %collective-permute-done.3.re_ref = f32[2,2,40,128]{3,2,1,0:T(8,128)S(1)} collective-permute-done((f32[2,2,40,128]{3,2,1,0:T(8,128)S(1)}, f32[2,2,40,128]{3,2,1,0:T(8,128)S(1)}, u32[]{:S(2)}, u32[]{:S(2)}) %collective-permute-start.3) | collective-permute-done | bytes 81952 | tf_op jit(solution)/shard_map/ppermute | solution.py:469
  9.3 2.7 %collective-permute-done.4.ro_ref = f32[2,2,40,128]{3,2,1,0:T(8,128)S(1)} collective-permute-done((f32[2,2,40,128]{3,2,1,0:T(8,128)S(1)}, f32[2,2,40,128]{3,2,1,0:T(8,128)S(1)}, u32[]{:S(2)}, u32[]{:S(2)}) %collective-permute-start.4) | collective-permute-done | bytes 81952 | tf_op jit(solution)/shard_map/ppermute | solution.py:469
  12.0 0.0 copy-done
  12.0 0.0 copy-done.1
  12.1 0.0 copy-done.4
  12.1 0.0 copy-done.5
  12.1 0.5 %shard_map.121 = (f32[4,16,128]{2,1,0:T(8,128)S(1)}, f32[4,4,16,128]{3,2,1,0:T(8,128)S(1)}, f32[4,2,32,128]{3,2,1,0:T(8,128)S(1)}, f32[4,2,16,128]{3,2,1,0:T(8,128)S(1)}, f32[4,2,16,128]{3,2,1,0:T(8,128)S(1)}) custom-call(f32[8,2,40,128]{3,2,1,0:T(8,128)S(1)} %get-tuple-element.28.ll_ref, f32[2,2,40,128]{3,2,1,0:T(8,128)S(1)} %collective-permute-done.3.re_ref, ...), custom_call_target="tpu_custom_call" | custom-call | flops 2000000 | bytes 2000000 | tf_op jit(solution)/shard_map/pallas_call | solution.py:541
  12.5 3.6 %collective-permute-start.9 = (f32[4,16,128]{2,1,0:T(8,128)S(1)}, f32[4,16,128]{2,1,0:T(8,128)S(1)}, u32[]{:S(2)}, u32[]{:S(2)}) collective-permute-start(f32[4,16,128]{2,1,0:T(8,128)S(1)} %get-tuple-element.35.own_ref.refs_0_), channel_id=1, source_target_pairs={{0,24},{1,25},{2,26},{3,27},{4,28},{5,29},{6,30},{7,31},{8,16},{9,... | collective-permute-start | bytes 98312 | tf_op jit(solution)/shard_map/ppermute | solution.py:469
  16.2 0.0 collective-permute-start.8
  16.2 0.8 %collective-permute-start.7 = (f32[4,16,128]{2,1,0:T(8,128)S(1)}, f32[4,16,128]{2,1,0:T(8,128)S(1)}, u32[]{:S(2)}, u32[]{:S(2)}) collective-permute-start(f32[4,16,128]{2,1,0:T(8,128)S(1)} %get-tuple-element.35.own_ref.refs_0_), channel_id=1, source_target_pairs={{0,8},{1,9},{2,10},{3,11},{4,12},{5,13},{6,14},{7,15},{8,0},{9,1},... | collective-permute-start | bytes 98312 | tf_op jit(solution)/shard_map/ppermute | solution.py:469
  16.9 1.6 %collective-permute-done.9.twelve_ref.refs_3_ = f32[4,16,128]{2,1,0:T(8,128)S(1)} collective-permute-done((f32[4,16,128]{2,1,0:T(8,128)S(1)}, f32[4,16,128]{2,1,0:T(8,128)S(1)}, u32[]{:S(2)}, u32[]{:S(2)}) %collective-permute-start.9) | collective-permute-done | bytes 32800 | tf_op jit(solution)/shard_map/ppermute | solution.py:469
  18.5 2.5 %collective-permute-done.8.eight_ref.refs_2_ = f32[4,16,128]{2,1,0:T(8,128)S(1)} collective-permute-done((f32[4,16,128]{2,1,0:T(8,128)S(1)}, f32[4,16,128]{2,1,0:T(8,128)S(1)}, u32[]{:S(2)}, u32[]{:S(2)}) %collective-permute-start.8) | collective-permute-done | bytes 32800 | tf_op jit(solution)/shard_map/ppermute | solution.py:469
  21.0 0.0 collective-permute-done.7.four_ref.refs_1_
  21.0 0.1 shard_map.124
  21.1 1.1 %collective-permute-start.10 = (f32[3,4,16,128]{3,2,1,0:T(8,128)S(1)}, f32[3,4,16,128]{3,2,1,0:T(8,128)S(1)}, u32[]{:S(2)}, u32[]{:S(2)}) collective-permute-start(f32[3,4,16,128]{3,2,1,0:T(8,128)S(1)} %get-tuple-element.36), channel_id=1, source_target_pairs={{0,2},{1,3},{2,0},{3,1},{4,6},{5,7},{6,4},{7,5},{8,10},{9,11},{10,... | collective-permute-start | bytes 294920 | tf_op jit(solution)/shard_map/ppermute | solution.py:469
  22.1 0.4 collective-permute-start.12
  22.5 2.1 %collective-permute-start.11 = (f32[3,4,16,128]{3,2,1,0:T(8,128)S(1)}, f32[3,4,16,128]{3,2,1,0:T(8,128)S(1)}, u32[]{:S(2)}, u32[]{:S(2)}) collective-permute-start(f32[3,4,16,128]{3,2,1,0:T(8,128)S(1)} %get-tuple-element.37), channel_id=1, source_target_pairs={{0,4},{1,5},{2,6},{3,7},{4,0},{5,1},{6,2},{7,3},{8,12},{9,13},{10,... | collective-permute-start | bytes 294920 | tf_op jit(solution)/shard_map/ppermute | solution.py:469
  24.6 1.0 %collective-permute-start.1 = (f32[3,2,2,32,128]{4,3,2,1,0:T(8,128)S(1)}, f32[3,2,2,32,128]{4,3,2,1,0:T(8,128)S(1)}, u32[]{:S(2)}, u32[]{:S(2)}) collective-permute-start(f32[3,2,2,32,128]{4,3,2,1,0:T(8,128)S(1)} %get-tuple-element.26), channel_id=1, source_target_pairs={{0,2},{1,3},{2,0},{3,1},{4,6},{5,7},{6,4},{7,5},{8,10},{9,11},{10,... | collective-permute-start | bytes 589832 | tf_op jit(solution)/shard_map/ppermute | solution.py:469
  25.6 0.5 %collective-permute-start.2 = (f32[3,2,2,32,128]{4,3,2,1,0:T(8,128)S(1)}, f32[3,2,2,32,128]{4,3,2,1,0:T(8,128)S(1)}, u32[]{:S(2)}, u32[]{:S(2)}) collective-permute-start(f32[3,2,2,32,128]{4,3,2,1,0:T(8,128)S(1)} %get-tuple-element.27), channel_id=1, source_target_pairs={{0,1},{1,0},{2,4},{3,5},{4,2},{5,3},{6,8},{7,9},{8,6},{9,7},{10,12... | collective-permute-start | bytes 589832 | tf_op jit(solution)/shard_map/ppermute | solution.py:469
  26.1 2.8 %collective-permute-done.10.refs_4_ = f32[3,4,16,128]{3,2,1,0:T(8,128)S(1)} collective-permute-done((f32[3,4,16,128]{3,2,1,0:T(8,128)S(1)}, f32[3,4,16,128]{3,2,1,0:T(8,128)S(1)}, u32[]{:S(2)}, u32[]{:S(2)}) %collective-permute-start.10) | collective-permute-done | bytes 98336 | tf_op jit(solution)/shard_map/ppermute | solution.py:469
  28.9 0.0 collective-permute-done.12.refs_6_
  28.9 0.0 collective-permute-done.11.refs_5_
  28.9 0.0 copy-done.2
  28.9 0.0 copy-done.3
  28.9 0.5 %shard_map.125.refs_0_ = f32[18,16,128]{2,1,0:T(8,128)S(1)} custom-call(f32[4,16,128]{2,1,0:T(8,128)S(1)} %get-tuple-element.35.own_ref.refs_0_, f32[4,16,128]{2,1,0:T(8,128)S(1)} %collective-permute-done.7.four_ref.refs_1_, f32[4,16,128]{2,1,0:T(8,128)S(1)} %collective-permute-done.8.eight_ref.refs_2_, ...), custom_call_target="tpu_custom_call" | custom-call | flops 2000000 | bytes 2000000 | tf_op jit(solution)/shard_map/pallas_call | solution.py:578
  29.4 0.1 collective-permute-start.13
  29.5 3.4 %collective-permute-start.5 = (f32[4,2,16,128]{3,2,1,0:T(8,128)S(1)}, f32[4,2,16,128]{3,2,1,0:T(8,128)S(1)}, u32[]{:S(2)}, u32[]{:S(2)}) collective-permute-start(f32[4,2,16,128]{3,2,1,0:T(8,128)S(1)} %get-tuple-element.33), channel_id=1, source_target_pairs={{0,2},{1,3},{2,0},{3,1},{4,6},{5,7},{6,4},{7,5},{8,10},{9,11},{10,... | collective-permute-start | bytes 196616 | tf_op jit(solution)/shard_map/ppermute | solution.py:469
  32.9 3.4 %collective-permute-start.6 = (f32[4,2,16,128]{3,2,1,0:T(8,128)S(1)}, f32[4,2,16,128]{3,2,1,0:T(8,128)S(1)}, u32[]{:S(2)}, u32[]{:S(2)}) collective-permute-start(f32[4,2,16,128]{3,2,1,0:T(8,128)S(1)} %get-tuple-element.34), channel_id=1, source_target_pairs={{0,1},{1,0},{2,4},{3,5},{4,2},{5,3},{6,8},{7,9},{8,6},{9,7},{10,12... | collective-permute-start | bytes 196616 | tf_op jit(solution)/shard_map/ppermute | solution.py:469
  36.3 0.0 collective-permute-done.5.re_ref
  36.3 3.8 %collective-permute-done.6.ro_ref = f32[4,2,16,128]{3,2,1,0:T(8,128)S(1)} collective-permute-done((f32[4,2,16,128]{3,2,1,0:T(8,128)S(1)}, f32[4,2,16,128]{3,2,1,0:T(8,128)S(1)}, u32[]{:S(2)}, u32[]{:S(2)}) %collective-permute-start.6) | collective-permute-done | bytes 65568 | tf_op jit(solution)/shard_map/ppermute | solution.py:469
  40.1 0.7 %shard_map.123 = f32[7,2,16,128]{3,2,1,0:T(8,128)} custom-call(f32[4,4,16,128]{3,2,1,0:T(8,128)S(1)} %get-tuple-element.32.d_ref, f32[4,2,16,128]{3,2,1,0:T(8,128)S(1)} %collective-permute-done.5.re_ref, f32[4,2,16,128]{3,2,1,0:T(8,128)S(1)} %collective-permute-done.6.ro_ref), custom_call_target="tpu_custom_call" | custom-call | flops 2000000 | bytes 2000000 | tf_op jit(solution)/shard_map/pallas_call | solution.py:584
  40.8 0.0 collective-permute-done.1.re_ref
  40.8 0.0 collective-permute-done.2.ro_ref
  40.8 1.2 %shard_map.122 = f32[7,4,32,256]{3,2,1,0:T(8,128)} custom-call(f32[3,8,2,32,128]{4,3,2,1,0:T(8,128)S(1)} %get-tuple-element.25.d_ref, f32[3,2,2,32,128]{4,3,2,1,0:T(8,128)S(1)} %collective-permute-done.1.re_ref, f32[3,2,2,32,128]{4,3,2,1,0:T(8,128)S(1)} %collective-permute-done.2.ro_ref, f32[4,2,32,128]{3,2,1,0:T(8,128)S(1)} %get-tuple-element.31.h_ref), custom_call_target="tpu_custom_call" | custom-call | flops 2000000 | bytes 2000000 | tf_op jit(solution)/shard_map/pallas_call | solution.py:583
  42.0 0.0 collective-permute-done.13.refs_1_
  42.0 1.1 %shard_map.126 = (f32[7,1,8,64]{3,2,1,0:T(8,128)}, f32[8,8,4,32]{3,2,1,0:T(4,128)}) custom-call(f32[18,16,128]{2,1,0:T(8,128)S(1)} %shard_map.125.refs_0_, f32[18,16,128]{2,1,0:T(8,128)S(1)} %collective-permute-done.13.refs_1_), custom_call_target="tpu_custom_call" | custom-call | flops 2000000 | bytes 2000000 | tf_op jit(solution)/shard_map/pallas_call | solution.py:590
Async XLA Ops:
  0.6 2.9 %collective-permute-start = (f32[8,64,512]{2,1,0:T(8,128)}, f32[8,64,512]{2,1,0:T(8,128)S(1)}, u32[]{:S(2)}, u32[]{:S(2)}) collective-permute-start(f32[8,64,512]{2,1,0:T(8,128)} %x_hbm.1), channel_id=1, source_target_pairs={{0,1},{1,0},{2,3},{3,2},{4,5},{5,4},{6,7},{7,6},{8,9},{9,8},{10,11... | collective-permute-start | bytes 3145736 | tf_op jit(solution)/shard_map/ppermute | solution.py:501
  3.6 8.5 %copy-start = (bf16[256,256]{1,0:T(8,128)(2,1)S(1)}, bf16[256,256]{1,0:T(8,128)(2,1)}, u32[]{:S(2)}) copy-start(bf16[256,256]{1,0:T(8,128)(2,1)} %constant.19.clone.tl_ref) | copy-start | bytes 393220
  3.6 8.5 %copy-start.1 = (bf16[256,256]{1,0:T(8,128)(2,1)S(1)}, bf16[256,256]{1,0:T(8,128)(2,1)}, u32[]{:S(2)}) copy-start(bf16[256,256]{1,0:T(8,128)(2,1)} %constant.18.clone.th_ref) | copy-start | bytes 393220
  3.6 8.5 %copy-start.4 = (bf16[128,128]{1,0:T(8,128)(2,1)S(1)}, bf16[128,128]{1,0:T(8,128)(2,1)}, u32[]{:S(2)}) copy-start(bf16[128,128]{1,0:T(8,128)(2,1)} %constant.21.clone.t3l_ref) | copy-start | bytes 98308
  3.6 8.5 %copy-start.5 = (bf16[128,128]{1,0:T(8,128)(2,1)S(1)}, bf16[128,128]{1,0:T(8,128)(2,1)}, u32[]{:S(2)}) copy-start(bf16[128,128]{1,0:T(8,128)(2,1)} %constant.20.clone.t3h_ref) | copy-start | bytes 98308
  3.6 25.3 %copy-start.2 = (bf16[128,128]{1,0:T(8,128)(2,1)S(1)}, bf16[128,128]{1,0:T(8,128)(2,1)}, u32[]{:S(2)}) copy-start(bf16[128,128]{1,0:T(8,128)(2,1)} %constant.23.clone.refs_8_) | copy-start | bytes 98308
  3.6 25.3 %copy-start.3 = (bf16[128,128]{1,0:T(8,128)(2,1)S(1)}, bf16[128,128]{1,0:T(8,128)(2,1)}, u32[]{:S(2)}) copy-start(bf16[128,128]{1,0:T(8,128)(2,1)} %constant.22.clone.refs_7_) | copy-start | bytes 98308
  4.7 4.6 %collective-permute-start.3 = (f32[2,2,40,128]{3,2,1,0:T(8,128)S(1)}, f32[2,2,40,128]{3,2,1,0:T(8,128)S(1)}, u32[]{:S(2)}, u32[]{:S(2)}) collective-permute-start(f32[2,2,40,128]{3,2,1,0:T(8,128)S(1)} %get-tuple-element.29), channel_id=1, source_target_pairs={{0,2},{1,3},{2,0},{3,1},{4,6},{5,7},{6,4},{7,5},{8,10},{9,11},{10,... | collective-permute-start | bytes 245768 | tf_op jit(solution)/shard_map/ppermute | solution.py:469
  4.8 7.2 %collective-permute-start.4 = (f32[2,2,40,128]{3,2,1,0:T(8,128)S(1)}, f32[2,2,40,128]{3,2,1,0:T(8,128)S(1)}, u32[]{:S(2)}, u32[]{:S(2)}) collective-permute-start(f32[2,2,40,128]{3,2,1,0:T(8,128)S(1)} %get-tuple-element.30), channel_id=1, source_target_pairs={{0,1},{1,0},{2,4},{3,5},{4,2},{5,3},{6,8},{7,9},{8,6},{9,7},{10,12... | collective-permute-start | bytes 245768 | tf_op jit(solution)/shard_map/ppermute | solution.py:469
  12.5 6.0 %collective-permute-start.9 = (f32[4,16,128]{2,1,0:T(8,128)S(1)}, f32[4,16,128]{2,1,0:T(8,128)S(1)}, u32[]{:S(2)}, u32[]{:S(2)}) collective-permute-start(f32[4,16,128]{2,1,0:T(8,128)S(1)} %get-tuple-element.35.own_ref.refs_0_), channel_id=1, source_target_pairs={{0,24},{1,25},{2,26},{3,27},{4,28},{5,29},{6,30},{7,31},{8,16},{9,... | collective-permute-start | bytes 98312 | tf_op jit(solution)/shard_map/ppermute | solution.py:469
  16.2 4.8 %collective-permute-start.8 = (f32[4,16,128]{2,1,0:T(8,128)S(1)}, f32[4,16,128]{2,1,0:T(8,128)S(1)}, u32[]{:S(2)}, u32[]{:S(2)}) collective-permute-start(f32[4,16,128]{2,1,0:T(8,128)S(1)} %get-tuple-element.35.own_ref.refs_0_), channel_id=1, source_target_pairs={{0,16},{1,17},{2,18},{3,19},{4,20},{5,21},{6,22},{7,23},{8,24},{9,... | collective-permute-start | bytes 98312 | tf_op jit(solution)/shard_map/ppermute | solution.py:469
  16.2 4.8 %collective-permute-start.7 = (f32[4,16,128]{2,1,0:T(8,128)S(1)}, f32[4,16,128]{2,1,0:T(8,128)S(1)}, u32[]{:S(2)}, u32[]{:S(2)}) collective-permute-start(f32[4,16,128]{2,1,0:T(8,128)S(1)} %get-tuple-element.35.own_ref.refs_0_), channel_id=1, source_target_pairs={{0,8},{1,9},{2,10},{3,11},{4,12},{5,13},{6,14},{7,15},{8,0},{9,1},... | collective-permute-start | bytes 98312 | tf_op jit(solution)/shard_map/ppermute | solution.py:469
  21.1 7.8 %collective-permute-start.10 = (f32[3,4,16,128]{3,2,1,0:T(8,128)S(1)}, f32[3,4,16,128]{3,2,1,0:T(8,128)S(1)}, u32[]{:S(2)}, u32[]{:S(2)}) collective-permute-start(f32[3,4,16,128]{3,2,1,0:T(8,128)S(1)} %get-tuple-element.36), channel_id=1, source_target_pairs={{0,2},{1,3},{2,0},{3,1},{4,6},{5,7},{6,4},{7,5},{8,10},{9,11},{10,... | collective-permute-start | bytes 294920 | tf_op jit(solution)/shard_map/ppermute | solution.py:469
  22.1 6.8 %collective-permute-start.12 = (f32[3,4,16,128]{3,2,1,0:T(8,128)S(1)}, f32[3,4,16,128]{3,2,1,0:T(8,128)S(1)}, u32[]{:S(2)}, u32[]{:S(2)}) collective-permute-start(f32[3,4,16,128]{3,2,1,0:T(8,128)S(1)} %get-tuple-element.37), channel_id=1, source_target_pairs={{0,6},{1,7},{2,4},{3,5},{4,2},{5,3},{6,0},{7,1},{8,14},{9,15},{10,... | collective-permute-start | bytes 294920 | tf_op jit(solution)/shard_map/ppermute | solution.py:469
  22.5 6.4 %collective-permute-start.11 = (f32[3,4,16,128]{3,2,1,0:T(8,128)S(1)}, f32[3,4,16,128]{3,2,1,0:T(8,128)S(1)}, u32[]{:S(2)}, u32[]{:S(2)}) collective-permute-start(f32[3,4,16,128]{3,2,1,0:T(8,128)S(1)} %get-tuple-element.37), channel_id=1, source_target_pairs={{0,4},{1,5},{2,6},{3,7},{4,0},{5,1},{6,2},{7,3},{8,12},{9,13},{10,... | collective-permute-start | bytes 294920 | tf_op jit(solution)/shard_map/ppermute | solution.py:469
  24.6 16.2 %collective-permute-start.1 = (f32[3,2,2,32,128]{4,3,2,1,0:T(8,128)S(1)}, f32[3,2,2,32,128]{4,3,2,1,0:T(8,128)S(1)}, u32[]{:S(2)}, u32[]{:S(2)}) collective-permute-start(f32[3,2,2,32,128]{4,3,2,1,0:T(8,128)S(1)} %get-tuple-element.26), channel_id=1, source_target_pairs={{0,2},{1,3},{2,0},{3,1},{4,6},{5,7},{6,4},{7,5},{8,10},{9,11},{10,... | collective-permute-start | bytes 589832 | tf_op jit(solution)/shard_map/ppermute | solution.py:469
  25.6 15.2 %collective-permute-start.2 = (f32[3,2,2,32,128]{4,3,2,1,0:T(8,128)S(1)}, f32[3,2,2,32,128]{4,3,2,1,0:T(8,128)S(1)}, u32[]{:S(2)}, u32[]{:S(2)}) collective-permute-start(f32[3,2,2,32,128]{4,3,2,1,0:T(8,128)S(1)} %get-tuple-element.27), channel_id=1, source_target_pairs={{0,1},{1,0},{2,4},{3,5},{4,2},{5,3},{6,8},{7,9},{8,6},{9,7},{10,12... | collective-permute-start | bytes 589832 | tf_op jit(solution)/shard_map/ppermute | solution.py:469
  29.4 12.6 %collective-permute-start.13 = (f32[18,16,128]{2,1,0:T(8,128)S(1)}, f32[18,16,128]{2,1,0:T(8,128)S(1)}, u32[]{:S(2)}, u32[]{:S(2)}) collective-permute-start(f32[18,16,128]{2,1,0:T(8,128)S(1)} %shard_map.125.refs_0_), channel_id=1, source_target_pairs={{0,1},{1,0},{2,3},{3,2},{4,5},{5,4},{6,7},{7,6},{8,9},{9,8},{10,11... | collective-permute-start | bytes 442376 | tf_op jit(solution)/shard_map/ppermute | solution.py:586
  29.5 6.8 %collective-permute-start.5 = (f32[4,2,16,128]{3,2,1,0:T(8,128)S(1)}, f32[4,2,16,128]{3,2,1,0:T(8,128)S(1)}, u32[]{:S(2)}, u32[]{:S(2)}) collective-permute-start(f32[4,2,16,128]{3,2,1,0:T(8,128)S(1)} %get-tuple-element.33), channel_id=1, source_target_pairs={{0,2},{1,3},{2,0},{3,1},{4,6},{5,7},{6,4},{7,5},{8,10},{9,11},{10,... | collective-permute-start | bytes 196616 | tf_op jit(solution)/shard_map/ppermute | solution.py:469
  32.9 7.2 %collective-permute-start.6 = (f32[4,2,16,128]{3,2,1,0:T(8,128)S(1)}, f32[4,2,16,128]{3,2,1,0:T(8,128)S(1)}, u32[]{:S(2)}, u32[]{:S(2)}) collective-permute-start(f32[4,2,16,128]{3,2,1,0:T(8,128)S(1)} %get-tuple-element.34), channel_id=1, source_target_pairs={{0,1},{1,0},{2,4},{3,5},{4,2},{5,3},{6,8},{7,9},{8,6},{9,7},{10,12... | collective-permute-start | bytes 196616 | tf_op jit(solution)/shard_map/ppermute | solution.py:469
